TPU v7x, 128 devices: a whole 4x4x4 slice. The times are simulated.
128 devices in a mesh: tm: 16 (over x, y_lo, core), space: 8 (over z, y_hi).
Axes of the slice: x: 4, y: 4 (y_hi: 2, y_lo: 2; y = y_hi * 2 + y_lo), z: 4, core: 2. Of those that a mesh axis runs over, the one named last changes fastest.
Arguments:
- input_field: float32 [64, 32, 32, 1024], P('tm', None, 'space'), may hold values from -6 to 6
- cotangent: float32 [64, 32, 32, 1024], P('tm', None, 'space'), may hold values from -6 to 6
- spectral_weights: float32 [2, 2, 16, 32, 32], replicated, may hold values from -0.75 to 0.75
- conv_kernel: float32 [2, 3, 32, 32], replicated, may hold values from -0.625 to 0.625
- mode_list: int32 [16], replicated, may hold values from 0 to 31, as said below
Outputs:
- grad_input: float32 [64, 32, 32, 1024], P('tm', None, 'space')
- grad_spectral: float32 [2, 2, 16, 32, 32], P(None, None, 'tm')
- grad_kernel: float32 [2, 3, 32, 32], replicated
Inputs may be any that keep to these rules, and one draw needn't show every extreme that they name: `mode_list`: 16 distinct frequencies in ascending order, with 0 and 31 among them.
All inputs are finite; a program needn't handle non-finite values.
Results may differ from a plain program's by a relative error of at most 0.00014.
Values sent between devices are 32-bit elements; how exact they have to be, the bound alone decides.
No kernel may reach another device: no remote copies, remote signals or barrier semaphores. Data moves between devices by JAX's collectives and lax.ppermute only.
A program may use at most 128 MiB of HBM per device.

v0:
```python
import functools
import math

import jax
import jax.numpy as jnp
from jax import lax
from jax.experimental import pallas as pl
from jax.experimental.pallas import tpu as pltpu
from jax.sharding import PartitionSpec as P

F32 = jnp.float32
BF16 = jnp.bfloat16
LANES = 128
J = 8
XB = 4
C = 32
VMEM = pl.BlockSpec(memory_space=pltpu.VMEM)
ANY = pl.BlockSpec(memory_space=pl.ANY)
HBM = pl.BlockSpec(memory_space=pltpu.HBM)
PARAMS = pltpu.CompilerParams(vmem_limit_bytes=40 * 1024 * 1024)


def in_hbm(*values):
    return [pltpu.with_memory_space_constraint(v, pltpu.HBM) for v in values]


def split(value):
    high = value.astype(BF16)
    low = (value - high.astype(F32)).astype(BF16)
    return high, low


def dot3(left, right, dims=((1,), (0,))):
    (lh, ll), (rh, rl) = left, right
    (lc,), (rc,) = dims
    a = jnp.concatenate([lh, ll, lh], axis=lc)
    b = jnp.concatenate([rh, rh, rl], axis=rc)
    return lax.dot_general(a, b, (dims, ((), ())), preferred_element_type=F32)


def scatter_kernel(field_any, out_any, field, out, load_sem, store_sem):
    steps, _, _, columns = field.shape
    groups = LANES // J
    loads = [
        pltpu.make_async_copy(field_any.at[t], field.at[t], load_sem.at[t]) for t in range(steps)
    ]
    for copy in loads:
        copy.start()
    stores = []
    for q in range(columns // LANES):
        lanes = slice(q * LANES, (q + 1) * LANES)
        part = pl.ds(q * groups, groups)
        for t in range(steps):
            if q == 0:
                loads[t].wait()
            rows = jnp.concatenate([field[t, :, x, lanes] for x in range(XB)], axis=0)
            out[part, t * J : (t + 1) * J] = rows.T.reshape(groups, J, LANES)
        stores.append(pltpu.make_async_copy(out.at[part], out_any.at[part], store_sem.at[q]))
        stores[-1].start()
    for copy in stores:
        copy.wait()


def gather_kernel(blocks_any, out_any, blocks, out, load_sem, store_sem):
    steps, _, _, columns = out.shape
    groups = LANES // J
    count = columns // LANES
    loads = []
    for q in range(count):
        part = pl.ds(q * groups, groups)
        loads.append(pltpu.make_async_copy(blocks_any.at[part], blocks.at[part], load_sem.at[q]))
        loads[-1].start()
    stores = []
    for q in range(count):
        lanes = slice(q * LANES, (q + 1) * LANES)
        loads[q].wait()
        for t in range(steps):
            rows = blocks[q * groups : (q + 1) * groups, t * J : (t + 1) * J]
            rows = rows.reshape(LANES, LANES).T
            for x in range(XB):
                out[t, :, x, lanes] = rows[x * C : (x + 1) * C]
        if q % 2 == 1:
            done = pl.ds((q - 1) * LANES, 2 * LANES)
            stores.append(
                pltpu.make_async_copy(
                    out.at[:, :, :, done], out_any.at[:, :, :, done], store_sem.at[q // 2]
                )
            )
            stores[-1].start()
    for copy in stores:
        copy.wait()


def to_blocks(field):
    steps, _, _, columns = field.shape
    shape = (columns // J, steps * J, LANES)
    return pl.pallas_call(
        scatter_kernel,
        in_specs=[HBM],
        out_specs=HBM,
        out_shape=pltpu.HBM(shape, F32),
        scratch_shapes=[
            pltpu.VMEM(field.shape, F32),
            pltpu.VMEM(shape, F32),
            pltpu.SemaphoreType.DMA((steps,)),
            pltpu.SemaphoreType.DMA((columns // LANES,)),
        ],
        compiler_params=PARAMS,
    )(*in_hbm(field))


def from_blocks(blocks):
    parts, rows, _ = blocks.shape
    shape = (rows // J, C, XB, parts * J)
    count = shape[3] // LANES
    return pl.pallas_call(
        gather_kernel,
        in_specs=[ANY],
        out_specs=HBM,
        out_shape=pltpu.HBM(shape, F32),
        scratch_shapes=[
            pltpu.VMEM(blocks.shape, F32),
            pltpu.VMEM(shape, F32),
            pltpu.SemaphoreType.DMA((count,)),
            pltpu.SemaphoreType.DMA((count // 2,)),
        ],
        compiler_params=PARAMS,
    )(blocks)


def angles(mode_list, total_time):
    steps = jnp.arange(total_time, dtype=jnp.int32)
    phase = (mode_list[:, None] * steps[None, :]) % total_time
    angle = phase.astype(F32) * (2.0 * math.pi / total_time)
    both = jnp.stack([jnp.cos(angle), -jnp.sin(angle)], axis=1)
    return both.reshape(2 * mode_list.shape[0], total_time)


def widened(value):
    rows, cols = value.shape
    spread = lax.broadcasted_iota(jnp.int32, (cols, cols * J), 1) // J
    spread = (spread == lax.broadcasted_iota(jnp.int32, (cols, cols * J), 0)).astype(BF16)
    shape = (rows * J, cols * J)
    same = (
        lax.broadcasted_iota(jnp.int32, shape, 0) % J
        == lax.broadcasted_iota(jnp.int32, shape, 1) % J
    )
    for piece in split(value):
        wide = jnp.dot(piece, spread, preferred_element_type=F32)
        wide = jnp.broadcast_to(wide[:, None, :], (rows, J, cols * J)).reshape(shape)
        yield jnp.where(same, wide, 0.0).astype(BF16)


def blocks_of(kernel, places, cols):
    zero = jnp.zeros((C, C), F32)
    rows = [
        jnp.concatenate([kernel[p[y]] if y in p else zero for y in range(cols)], axis=1)
        for p in places
    ]
    return jnp.concatenate(rows, axis=0)


def band(kernel):
    cells = 2 * XB
    own = [{y: x - y + 1 for y in range(cells) if abs(x - y) <= 1} for x in range(cells)]
    before, after = {0: 0}, {cells - 1: 2}
    own = split(blocks_of(kernel, own, cells))
    both = split(blocks_of(kernel, [after, before, after, before], cells))
    edge = split(blocks_of(kernel, [after, {}, {}, before], cells))
    return jnp.concatenate([own[0], own[0], own[1], both[0], edge[1]], axis=0)


def prepare_kernel(scale, tab_ref, tabt_ref, w_ref, k_ref, ah, al, sh, sl, wh, wl, vh, vl, fb, bb):
    ah[...], al[...] = widened(tab_ref[...])
    sh[...], sl[...] = widened(tabt_ref[...])
    for l in range(w_ref.shape[0]):

        def body(m, _):
            re, im = w_ref[l, 0, m] * scale, w_ref[l, 1, m] * scale
            wh[l, m], wl[l, m] = split(jnp.concatenate([re] * XB + [im] * XB, axis=1))
            re, im = re.T, -im.T
            vh[l, m], vl[l, m] = split(jnp.concatenate([re] * XB + [im] * XB, axis=1))
            return 0

        lax.fori_loop(0, w_ref.shape[2], body, 0)
        taps = [k_ref[l, j] for j in range(3)]
        fb[l] = band(taps)
        bb[l] = band([t.T for t in taps[::-1]])


def prepare(scale, spectral_weights, conv_kernel, mode_list, total_time):
    layers, _, modes, channels, _ = spectral_weights.shape
    tab = angles(mode_list, total_time)
    rows, cols = 2 * modes * J, total_time * J
    shapes = [(rows, cols)] * 2 + [(cols, rows)] * 2
    shapes += [(layers, modes, channels, 2 * LANES)] * 4 + [(layers, 8 * LANES, 2 * LANES)] * 2
    return pl.pallas_call(
        functools.partial(prepare_kernel, scale),
        in_specs=[VMEM] * 4,
        out_specs=[VMEM] * 10,
        out_shape=[pltpu.HBM(shape, BF16) for shape in shapes],
        compiler_params=PARAMS,
    )(tab, tab.T, spectral_weights, conv_kernel)


def lane_block():
    return lax.broadcasted_iota(jnp.int32, (1, LANES), 1) // C


def put_split(value, s, high_ref, low_ref):
    high, low = split(value)
    high_ref[s] = high
    low_ref[s] = low


def with_neighbours(ref, s):
    own = ref[s]
    x = lane_block()
    zero = jnp.zeros_like(own)
    before = ref[s - 1] if s > 0 else zero
    after = ref[s + 1] if s + 1 < ref.shape[0] else zero
    edge = jnp.where(x == XB - 1, before, jnp.where(x == 0, after, zero))
    return jnp.concatenate([own, edge], axis=1)


def pair_operand(high_ref, low_ref, s):
    x = lane_block()
    bricks = high_ref.shape[0]

    def edges(ref):
        zero = jnp.zeros_like(ref[s])
        before = ref[s - 1] if s > 0 else zero
        after = ref[s + 2] if s + 2 < bricks else zero
        return jnp.where(x == XB - 1, before, jnp.where(x == 0, after, zero))

    high = [high_ref[s], high_ref[s + 1]]
    low = [low_ref[s], low_ref[s + 1]]
    edge, edge_low = edges(high_ref), edges(low_ref)
    half = LANES // 2
    swapped = jnp.concatenate([edge_low[:, half:], edge_low[:, :half]], axis=1)
    both = jnp.where((x == 0) | (x == XB - 1), edge, swapped)
    return jnp.concatenate([*high, *low, *high, both, edge], axis=1)


def analyse_pair(table, high_ref, low_ref, coef_ref, s):
    right = [jnp.concatenate([r[s], r[s + 1]], axis=1) for r in (high_ref, low_ref)]
    result = dot3(table, right)
    coef_ref[s] = result[:, :LANES]
    coef_ref[s + 1] = result[:, LANES:]


def analyse(table, high_ref, low_ref, coef_ref):
    for s in range(0, high_ref.shape[0], 2):
        analyse_pair(table, high_ref, low_ref, coef_ref, s)


def mixing_matrix(w_ref, l, m):
    row = lax.broadcasted_iota(jnp.int32, (LANES, 2 * LANES), 0) // C
    col = lax.broadcasted_iota(jnp.int32, (LANES, 2 * LANES), 1) // C % XB
    wide = jnp.concatenate([w_ref[l, m]] * XB, axis=0)
    top = jnp.where(row == col, wide, jnp.zeros_like(wide))
    return jnp.concatenate(
        [top, jnp.concatenate([-top[:, LANES:], top[:, :LANES]], axis=1)], axis=0
    )


def mix(coef_ref, wh_ref, wl_ref, l, mixed_ref):
    bricks = coef_ref.shape[0]
    for m in range(wh_ref.shape[1]):
        re, im = slice(2 * J * m, 2 * J * m + J), slice(2 * J * m + J, 2 * J * (m + 1))
        value = jnp.concatenate(
            [coef_ref[:, re].reshape(bricks * J, LANES), coef_ref[:, im].reshape(bricks * J, LANES)],
            axis=1,
        )
        matrix = (mixing_matrix(wh_ref, l, m), mixing_matrix(wl_ref, l, m))
        result = dot3(split(value), matrix)
        mixed_ref[:, re] = result[:, :LANES].reshape(bricks, J, LANES)
        mixed_ref[:, im] = result[:, LANES:].reshape(bricks, J, LANES)


def synthesise(table, mixed_ref, matrix, high_ref, low_ref, emit):
    for s in range(0, mixed_ref.shape[0], 2):
        right = split(jnp.concatenate([mixed_ref[s], mixed_ref[s + 1]], axis=1))
        total = dot3(table, right) + jnp.dot(
            pair_operand(high_ref, low_ref, s), matrix, preferred_element_type=F32
        )
        emit(s, total[:, :LANES])
        emit(s + 1, total[:, LANES:])


def gelu_parts(z):
    cdf = 0.5 * (1.0 + lax.erf(z * math.sqrt(0.5)))
    slope = cdf + z * (jnp.exp(-0.5 * z * z) * (1.0 / math.sqrt(2.0 * math.pi)))
    return z * cdf, slope


def brick(ref, s):
    return ref[:, s].reshape(-1, LANES)


def forward_kernel(
    x_ref, ah, al, sh, sl, wh, wl, fb,
    coef1, coef2, slope1, slope2, x1h, x1l, x2h, x2l, mixed,
):
    bricks = x_ref.shape[1]
    for s in range(bricks):
        put_split(brick(x_ref, s), s, x1h, x1l)
    analysis, synthesis = (ah[...], al[...]), (sh[...], sl[...])

    def first(s, z):
        value, slope = gelu_parts(z)
        slope1[s] = slope
        put_split(value, s, x2h, x2l)

    def second(s, z):
        slope2[s] = gelu_parts(z)[1]

    for l, (h, low, coef, emit) in enumerate(
        ((x1h, x1l, coef1, first), (x2h, x2l, coef2, second))
    ):
        analyse(analysis, h, low, coef)
        mix(coef, wh, wl, l, mixed)
        synthesise(synthesis, mixed, fb[l], h, low, emit)


def forward(field, tabs, weights, bands_):
    _, bricks, _, _ = field.shape
    rows = tabs[0].shape[1]
    modes = tabs[0].shape[0]
    coef = pltpu.HBM((bricks, modes, LANES), F32)
    full = pltpu.HBM((bricks, rows, LANES), F32)
    half = pltpu.HBM((bricks, rows, LANES), BF16)
    return pl.pallas_call(
        forward_kernel,
        in_specs=[VMEM] * 8,
        out_specs=[VMEM] * 8,
        out_shape=[coef, coef, full, full, half, half, half, half],
        scratch_shapes=[pltpu.VMEM((bricks, modes, LANES), F32)],
        compiler_params=PARAMS,
    )(field, *in_hbm(*tabs, *weights, *bands_))


def backward_kernel(*refs):
    g_any, slope1_any, slope2_any = refs[:3]
    small_any = refs[3:10]
    out_any, sens1_any, sens2_any = refs[10:13]
    z_any = refs[13:17]
    g, slope1, slope2 = refs[17:20]
    small = refs[20:27]
    sens1, sens2, z1h, z1l, z2h, z2l, out, mixed, load_sem, small_sem, store_sem = refs[27:]
    ah, al, sh, sl, wh, wl, bb = small
    bricks = g.shape[0]
    copy = pltpu.make_async_copy

    loads = [
        (
            copy(g_any.at[:, s], g.at[s], load_sem.at[0, s]),
            copy(slope2_any.at[s], slope2.at[s], load_sem.at[1, s]),
            copy(slope1_any.at[s], slope1.at[s], load_sem.at[2, s]),
        )
        for s in range(bricks)
    ]
    tables = [copy(a, r, small_sem.at[i]) for i, (a, r) in enumerate(zip(small_any, small))]
    for s in range(bricks):
        loads[s][0].start()
        loads[s][1].start()
        if s == 1:
            tables[0].start()
            tables[1].start()
    for i in (4, 5, 2, 3, 6):
        tables[i].start()
    for s in range(bricks):
        loads[s][2].start()

    stores = []

    def store(source, target):
        stores.append(copy(source, target, store_sem.at[len(stores)]))
        stores[-1].start()

    for s in range(0, bricks, 2):
        for o in (s, s + 1):
            loads[o][0].wait()
            loads[o][1].wait()
        if s == 0:
            tables[0].wait()
            tables[1].wait()
        for o in (s, s + 1):
            put_split(g[o].reshape(-1, LANES) * slope2[o], o, z2h, z2l)
        analyse_pair((ah[...], al[...]), z2h, z2l, sens2, s)
    store(z2h, z_any[2])
    store(z2l, z_any[3])
    store(sens2, sens2_any)
    for i in range(2, 7):
        tables[i].wait()
    analysis, synthesis = (ah[...], al[...]), (sh[...], sl[...])

    def second(s, value):
        loads[s][2].wait()
        put_split(value * slope1[s], s, z1h, z1l)

    def first(s, value):
        out[s] = value.reshape(out.shape[1:])
        store(out.at[s], out_any.at[:, s])

    mix(sens2, wh, wl, 1, mixed)
    synthesise(synthesis, mixed, bb[1], z2h, z2l, second)
    store(z1h, z_any[0])
    store(z1l, z_any[1])
    analyse(analysis, z1h, z1l, sens1)
    store(sens1, sens1_any)
    mix(sens1, wh, wl, 0, mixed)
    synthesise(synthesis, mixed, bb[0], z1h, z1l, first)
    for done in stores:
        done.wait()


def backward(cotangent, slope1, slope2, tabs, weights, bands_):
    groups, bricks, lines, _ = cotangent.shape
    rows = tabs[0].shape[1]
    modes = tabs[0].shape[0]
    coef = ((bricks, modes, LANES), F32)
    half = ((bricks, rows, LANES), BF16)
    brick_shape = ((bricks, groups, lines, LANES), F32)
    outs = [(cotangent.shape, F32), coef, coef, half, half, half, half]
    operands = (cotangent, slope1, slope2, *tabs, *weights, *bands_)
    scratch = [brick_shape] + [(o.shape, o.dtype) for o in operands[1:]]
    scratch += [coef, coef, half, half, half, half, brick_shape, coef]
    return pl.pallas_call(
        backward_kernel,
        in_specs=[ANY] + [HBM] * 9,
        out_specs=[HBM] * 7,
        out_shape=[pltpu.HBM(*o) for o in outs],
        scratch_shapes=[pltpu.VMEM(*o) for o in scratch]
        + [
            pltpu.SemaphoreType.DMA((3, bricks)),
            pltpu.SemaphoreType.DMA((7,)),
            pltpu.SemaphoreType.DMA((6 + bricks,)),
        ],
        compiler_params=PARAMS,
    )(cotangent, *in_hbm(*operands[1:]))


ROWS = ((0,), (0,))
TAPS = 3
RADIX = 4


def weight_kernel(scale, me_ref, *refs):
    coef1_any, coef2_any, sens1_any, sens2_any = refs[:4]
    half_any = refs[4:12]
    modes = refs[0].shape[1] // (2 * J)
    outs = refs[12 : 12 + RADIX]
    coef1, coef2, sens1, sens2 = refs[12 + RADIX : 16 + RADIX]
    half = refs[16 + RADIX : 24 + RADIX]
    spectral, load_sem, half_sem = refs[24 + RADIX :]
    bricks = coef1.shape[0]
    copy = pltpu.make_async_copy

    halves = [
        [
            copy(a.at[s], r.at[s], half_sem.at[i, s])
            for i, (a, r) in enumerate(zip(half_any, half))
        ]
        for s in range(bricks)
    ]
    pairs = zip((coef1_any, coef2_any, sens1_any, sens2_any), (coef1, coef2, sens1, sens2))
    loads = [copy(a, r, load_sem.at[i]) for i, (a, r) in enumerate(pairs)]
    x1h, x1l, x2h, x2l, z1h, z1l, z2h, z2l = half
    for l in range(2):
        for s in range(bricks):
            for i in (0, 1, 4, 5) if l == 0 else (2, 3, 6, 7):
                halves[s][i].start()
    for c in loads:
        c.start()

    blocks = []
    for l, (xh, xl, zh, zl) in enumerate(((x1h, x1l, z1h, z1l), (x2h, x2l, z2h, z2l))):
        total = jnp.zeros((LANES, 2 * LANES), F32)
        for s in range(bricks):
            for ahead in (0, 1) if s == 0 else (s + 1,):
                if ahead < bricks:
                    for i in (0, 1, 4, 5) if l == 0 else (2, 3, 6, 7):
                        halves[ahead][i].wait()
            value = (with_neighbours(xh, s), with_neighbours(xl, s))
            total = total + dot3((zh[s], zl[s]), value, ROWS)
        for j in range(TAPS):
            pairs = [(x, x - j + 1) for x in range(XB) if 0 <= x - j + 1 < XB]
            tap = sum(total[y * C : (y + 1) * C, x * C : (x + 1) * C] for x, y in pairs)
            if j == 0:
                tap = tap + total[:C, LANES + (XB - 1) * C :]
            if j == 2:
                tap = tap + total[(XB - 1) * C :, LANES : LANES + C]
            blocks.append(tap)
    half_rows = C // 2
    first = jnp.concatenate(blocks[:4], axis=1)
    rest = [b[i * half_rows : (i + 1) * half_rows] for b in blocks[4:] for i in range(2)]
    kernels = jnp.concatenate([first, jnp.concatenate(rest, axis=1)], axis=0)

    for c in loads:
        c.wait()
    for m in range(modes):
        re, im = slice(2 * J * m, 2 * J * m + J), slice(2 * J * m + J, 2 * J * (m + 1))
        pieces = []
        for coef, sens in ((coef1, sens1), (coef2, sens2)):
            cr, ci, zr, zi = (
                r[:, p].reshape(bricks * J, LANES)
                for r, p in ((coef, re), (coef, im), (sens, re), (sens, im))
            )
            left = jnp.concatenate([cr, ci], axis=0)
            right = jnp.concatenate(
                [jnp.concatenate([zr, zi], axis=1), jnp.concatenate([zi, -zr], axis=1)], axis=0
            )
            product = dot3(split(left), split(right), ROWS) * scale
            for part in range(2):
                pieces.append(
                    sum(
                        product[x * C : (x + 1) * C, part * LANES + x * C : part * LANES + (x + 1) * C]
                        for x in range(XB)
                    )
                )
        spectral[m] = jnp.concatenate(pieces, axis=1)
    for r, out in enumerate(outs):
        high = (me_ref[0] + r) % RADIX
        for q in range(RADIX):
            low = (me_ref[1] + q) % RADIX
            out[q * C : (q + 1) * C] = spectral[high * RADIX + low]
        out[RADIX * C :] = kernels


def weight_gradients(scale, me, *operands):
    modes = operands[0].shape[1] // (2 * J)
    rows = RADIX * C + 2 * TAPS * C // XB
    return pl.pallas_call(
        functools.partial(weight_kernel, scale),
        in_specs=[pl.BlockSpec(memory_space=pltpu.SMEM)] + [HBM] * 12,
        out_specs=[VMEM] * RADIX,
        out_shape=[jax.ShapeDtypeStruct((rows, LANES), F32)] * RADIX,
        scratch_shapes=[pltpu.VMEM(o.shape, o.dtype) for o in operands]
        + [
            pltpu.VMEM((modes, C, LANES), F32),
            pltpu.SemaphoreType.DMA((4,)),
            pltpu.SemaphoreType.DMA((8, operands[0].shape[0])),
        ],
        compiler_params=PARAMS,
    )(me, *in_hbm(*operands))


def shifted(pieces, axis, size, stride):
    count = len(pieces)
    got = [pieces[0]]
    for r in range(1, count):
        perm = []
        for i in range(size):
            digit = i // stride % count
            perm.append((i, i + ((digit + r) % count - digit) * stride))
        got.append(lax.ppermute(pieces[r], axis, perm))
    return got


def ring_sum(values):
    while len(values) > 1:
        half = len(values) // 2
        values = [values[i] + values[i + half] for i in range(half)]
    return values[0]


def split_sum_kernel(*refs):
    total = ring_sum([r[...] for r in refs[:RADIX]])
    for q, out in enumerate(refs[RADIX:]):
        out[:C] = total[q * C : (q + 1) * C]
        out[C:] = total[RADIX * C :]


def split_sum(pieces):
    rows = pieces[0].shape[0] - (RADIX - 1) * C
    return pl.pallas_call(
        split_sum_kernel,
        in_specs=[VMEM] * RADIX,
        out_specs=[VMEM] * RADIX,
        out_shape=[jax.ShapeDtypeStruct((rows, LANES), F32)] * RADIX,
        compiler_params=PARAMS,
    )(*pieces)


def finish_kernel(one_ref, other_ref, mode_ref, kernel_ref):
    total = one_ref[...] + other_ref[...]
    layers = mode_ref.shape[0]
    for l in range(layers):
        for part in range(2):
            at = (2 * l + part) * C
            mode_ref[l, part, 0] = total[:C, at : at + C]
    low = C // 2
    blocks = [total[C : 2 * C, b * C : (b + 1) * C] for b in range(XB)]
    for b in range(2):
        top, bottom = (total[2 * C :, (2 * b + i) * C : (2 * b + i + 1) * C] for i in range(2))
        blocks.append(jnp.concatenate([top, bottom], axis=0))
    for i, block in enumerate(blocks):
        kernel_ref[i // TAPS, i % TAPS] = block.T


def finish(one, other, layers):
    return pl.pallas_call(
        finish_kernel,
        in_specs=[VMEM] * 2,
        out_specs=[VMEM] * 2,
        out_shape=[
            jax.ShapeDtypeStruct((layers, 2, 1, C, C), F32),
            jax.ShapeDtypeStruct((layers, TAPS, C, C), F32),
        ],
        compiler_params=PARAMS,
    )(one, other)


def on_device(input_field, cotangent, spectral_weights, conv_kernel, mode_list):
    groups = lax.axis_size("tm")
    bricks = lax.axis_size("space")
    everyone = ("tm", "space")
    steps = input_field.shape[0]
    total_time = steps * groups
    layers, _, modes, _, _ = spectral_weights.shape
    scale = 2.0 / total_time
    exchange = functools.partial(lax.all_to_all, split_axis=0, concat_axis=0, tiled=True)

    received = exchange(to_blocks(input_field), everyone)
    cot_blocks = to_blocks(cotangent)
    prepared = prepare(scale, spectral_weights, conv_kernel, mode_list, total_time)
    received, cot_blocks, prepared = lax.optimization_barrier((received, cot_blocks, prepared))
    tabs = prepared[:4]
    cot_received = exchange(cot_blocks, everyone)
    shape = (groups, bricks, steps * J, LANES)
    coef1, coef2, slope1, slope2, x1h, x1l, x2h, x2l = forward(
        received.reshape(shape), tabs, prepared[4:6], prepared[8:9]
    )
    grad, sens1, sens2, z1h, z1l, z2h, z2l = backward(
        cot_received.reshape(shape), slope1, slope2, tabs, prepared[6:8], prepared[9:]
    )
    returned = exchange(grad.reshape(cot_received.shape), everyone)
    me = lax.axis_index("tm").astype(jnp.int32)
    place = jnp.stack([me // RADIX, me % RADIX])
    pieces = weight_gradients(
        scale, place, coef1, coef2, sens1, sens2, x1h, x1l, x2h, x2l, z1h, z1l, z2h, z2l
    )
    pieces = split_sum(shifted(pieces, "tm", groups, RADIX))
    grad_input, pieces = lax.optimization_barrier(
        (from_blocks(returned), shifted(pieces, "tm", groups, 1))
    )
    total = ring_sum(pieces)
    total = ring_sum(shifted([total] * RADIX, "space", bricks, bricks // RADIX))
    mode_total, kernel_total = finish(*shifted([total] * 2, "space", bricks, 1), layers)
    return (grad_input, mode_total, kernel_total)


def solution(mesh):
    placed = (P("tm", None, "space", None), P("tm", None, "space", None), P(), P(), P())
    return jax.shard_map(
        on_device,
        mesh=mesh,
        in_specs=placed,
        out_specs=(P("tm", None, "space", None), P(None, None, "tm", None, None), P()),
        check_vma=False,
    )
```

profile of v0, /device:TPU:0, one launch (start us, length us, event | category | flops | bytes accessed | tf_op | source)
XLA Modules:
  0.0 151.9 jit_solution(17614146693428836362)
XLA Ops:
  0.6 3.8 %shard_map.76 = f32[128,32,128]{2,1,0:T(8,128)} custom-call(f32[4,32,4,1024]{3,2,1,0:T(4,128)} %field_any.2), custom_call_target="tpu_custom_call" | custom-call | tf_op jit(solution)/shard_map/pallas_call | solution.py:97
  4.4 0.0 copy-start.2
  4.4 11.1 %all-to-all-start = ((f32[128,32,128]{2,1,0:T(8,128)}), f32[128,32,128]{2,1,0:T(8,128)S(1)}, u32[]{:S(2)}, u32[]{:S(2)}) async-start(f32[128,32,128]{2,1,0:T(8,128)} %shard_map.76), calls=%async_computation | async-start | bytes 4194304 | tf_op jit(solution)/shard_map/all_to_all | solution.py:625
  15.6 0.0 copy-done.2
  15.6 0.1 fusion.6
  15.7 0.1 copy.11
  15.8 0.0 copy-start
  15.8 0.0 copy-start.1
  15.8 3.9 %shard_map.77 = f32[128,32,128]{2,1,0:T(8,128)} custom-call(f32[4,32,4,1024]{3,2,1,0:T(4,128)} %field_any.3), custom_call_target="tpu_custom_call" | custom-call | tf_op jit(solution)/shard_map/pallas_call | solution.py:97
  19.7 0.0 copy-done
  19.7 0.0 copy-done.1
  19.7 8.7 %shard_map.78 = (bf16[256,512]{1,0:T(8,128)(2,1)}, bf16[256,512]{1,0:T(8,128)(2,1)}, bf16[512,256]{1,0:T(8,128)(2,1)}, bf16[512,256]{1,0:T(8,128)(2,1)}, bf16[2,...) custom-call(f32[32,64]{1,0:T(8,128)S(1)} %bitcast.9, ...), custom_call_target="tpu_custom_call" | custom-call | tf_op jit(solution)/shard_map/pallas_call | solution.py:197
  28.5 16.3 %all-to-all-done = f32[128,32,128]{2,1,0:T(8,128)S(1)} async-done(((f32[128,32,128]{2,1,0:T(8,128)}), f32[128,32,128]{2,1,0:T(8,128)S(1)}, u32[]{:S(2)}, u32[]{:S(2)}) %all-to-all-start) | async-done | bytes 2097184 | tf_op jit(solution)/shard_map/all_to_all | solution.py:625
  44.7 6.0 %all-to-all-start.1 = ((f32[128,32,128]{2,1,0:T(8,128)}), f32[128,32,128]{2,1,0:T(8,128)}, u32[]{:S(2)}, u32[]{:S(2)}) async-start(f32[128,32,128]{2,1,0:T(8,128)} %shard_map.77), calls=%async_computation.1 | async-start | bytes 4194304 | tf_op jit(solution)/shard_map/all_to_all | solution.py:630
  50.7 12.2 %shard_map.79 = (f32[8,256,128]{2,1,0:T(8,128)}, f32[8,256,128]{2,1,0:T(8,128)}, f32[8,512,128]{2,1,0:T(8,128)}, f32[8,512,128]{2,1,0:T(8,128)}, bf16[8,512,128]...) custom-call(f32[16,8,32,128]{3,2,1,0:T(8,128)S(1)} %bitcast.7, ...), custom_call_target="tpu_custom_call" | custom-call | tf_op jit(solution)/shard_map/pallas_call | solution.py:333
  62.9 16.3 %all-to-all-done.1 = f32[128,32,128]{2,1,0:T(8,128)} async-done(((f32[128,32,128]{2,1,0:T(8,128)}), f32[128,32,128]{2,1,0:T(8,128)}, u32[]{:S(2)}, u32[]{:S(2)}) %all-to-all-start.1) | async-done | bytes 2097184 | tf_op jit(solution)/shard_map/all_to_all | solution.py:630
  79.3 16.1 %shard_map.80 = (f32[16,8,32,128]{3,2,1,0:T(8,128)}, f32[8,256,128]{2,1,0:T(8,128)}, f32[8,256,128]{2,1,0:T(8,128)}, bf16[8,512,128]{2,1,0:T(8,128)(2,1)}, bf16[...) custom-call(f32[16,8,32,128]{3,2,1,0:T(8,128)} %bitcast.2.refs_0_, ...), custom_call_target="tpu_custom_call" | custom-call | tf_op jit(solution)/shard_map/pallas_call | solution.py:429
  95.4 5.3 %all-to-all-start.2 = ((f32[128,32,128]{2,1,0:T(8,128)}), f32[128,32,128]{2,1,0:T(8,128)S(1)}, u32[]{:S(2)}, u32[]{:S(2)}) async-start(f32[128,32,128]{2,1,0:T(8,128)} %bitcast.11), calls=%async_computation.2 | async-start | bytes 4194304 | tf_op jit(solution)/shard_map/all_to_all | solution.py:638
  100.7 0.1 pad_add_fusion.me_ref
  100.8 9.7 %shard_map.82 = (f32[176,128]{1,0:T(8,128)S(1)}, f32[176,128]{1,0:T(8,128)S(1)}, f32[176,128]{1,0:T(8,128)S(1)}, f32[176,128]{1,0:T(8,128)S(1)}) custom-call(s32[2]{0:T(128)S(1)} %pad_add_fusion.me_ref, f32[8,256,128]{2,1,0:T(8,128)} %get-tuple-element.80.refs_0_, f32[8,256,128]{2,1,0:T(8,128)} %get-tuple-element.81.refs_1_, ...), custom_call_target="tpu_custom_call" | custom-call | tf_op jit(solution)/shard_map/pallas_call | solution.py:534
  110.5 1.0 collective-permute-start
  111.5 2.7 %collective-permute-start.1 = (f32[176,128]{1,0:T(8,128)S(1)}, f32[176,128]{1,0:T(8,128)S(1)}, u32[]{:S(2)}, u32[]{:S(2)}) collective-permute-start(f32[176,128]{1,0:T(8,128)S(1)} %get-tuple-element.94), channel_id=1, source_target_pairs={{0,64},{8,72},{16,80},{24,88},{32,96},{40,104},{48,112},{56,120},{... | collective-permute-start | bytes 270344 | tf_op jit(solution)/shard_map/ppermute | solution.py:557
  114.2 1.5 collective-permute-start.2
  115.7 12.1 %collective-permute-done.refs_1_ = f32[176,128]{1,0:T(8,128)S(1)} collective-permute-done((f32[176,128]{1,0:T(8,128)S(1)}, f32[176,128]{1,0:T(8,128)S(1)}, u32[]{:S(2)}, u32[]{:S(2)}) %collective-permute-start) | collective-permute-done | bytes 90144 | tf_op jit(solution)/shard_map/ppermute | solution.py:557
  127.8 2.0 %collective-permute-done.1.refs_2_ = f32[176,128]{1,0:T(8,128)S(1)} collective-permute-done((f32[176,128]{1,0:T(8,128)S(1)}, f32[176,128]{1,0:T(8,128)S(1)}, u32[]{:S(2)}, u32[]{:S(2)}) %collective-permute-start.1) | collective-permute-done | bytes 90144 | tf_op jit(solution)/shard_map/ppermute | solution.py:557
  129.8 0.0 collective-permute-done.2.refs_3_
  129.9 0.1 collective-permute-start.3
  129.9 1.5 %collective-permute-start.4 = (f32[80,128]{1,0:T(8,128)S(1)}, f32[80,128]{1,0:T(8,128)S(1)}, u32[]{:S(2)}, u32[]{:S(2)}) collective-permute-start(f32[80,128]{1,0:T(8,128)S(1)} %get-tuple-element.98), channel_id=1, source_target_pairs={{0,16},{8,24},{16,0},{24,8},{32,48},{40,56},{48,32},{56,40},{64,80... | collective-permute-start | bytes 122888 | tf_op jit(solution)/shard_map/ppermute | solution.py:557
  131.5 1.4 collective-permute-start.5
  132.9 0.0 all-to-all-done.2.blocks_any
  132.9 3.7 %shard_map.81 = f32[4,32,4,1024]{3,2,1,0:T(4,128)} custom-call(f32[128,32,128]{2,1,0:T(8,128)S(1)} %all-to-all-done.2.blocks_any), custom_call_target="tpu_custom_call" | custom-call | tf_op jit(solution)/shard_map/pallas_call | solution.py:116
  136.6 0.0 collective-permute-done.3
  136.6 0.0 collective-permute-done.4
  136.6 0.0 collective-permute-done.5
  136.6 3.5 %collective-permute-start.6 = (f32[80,128]{1,0:T(8,128)S(1)}, f32[80,128]{1,0:T(8,128)S(1)}, u32[]{:S(2)}, u32[]{:S(2)}) collective-permute-start(f32[80,128]{1,0:T(8,128)S(1)} %add_add_fusion.1), channel_id=1, source_target_pairs={{0,4},{1,5},{2,6},{3,7},{4,0},{5,1},{6,2},{7,3},{8,12},{9,13},{10,... | collective-permute-start | bytes 122888 | tf_op jit(solution)/shard_map/ppermute | solution.py:557
  140.2 0.8 collective-permute-start.7
  141.0 2.4 %collective-permute-start.8 = (f32[80,128]{1,0:T(8,128)S(1)}, f32[80,128]{1,0:T(8,128)S(1)}, u32[]{:S(2)}, u32[]{:S(2)}) collective-permute-start(f32[80,128]{1,0:T(8,128)S(1)} %add_add_fusion.1), channel_id=1, source_target_pairs={{0,6},{1,7},{2,0},{3,1},{4,2},{5,3},{6,4},{7,5},{8,14},{9,15},{10,... | collective-permute-start | bytes 122888 | tf_op jit(solution)/shard_map/ppermute | solution.py:557
  143.4 0.0 collective-permute-done.6
  143.4 2.0 %collective-permute-done.7 = f32[80,128]{1,0:T(8,128)S(1)} collective-permute-done((f32[80,128]{1,0:T(8,128)S(1)}, f32[80,128]{1,0:T(8,128)S(1)}, u32[]{:S(2)}, u32[]{:S(2)}) %collective-permute-start.7) | collective-permute-done | bytes 40992 | tf_op jit(solution)/shard_map/ppermute | solution.py:557
  145.4 0.0 collective-permute-done.8
  145.4 2.9 %collective-permute-start.9 = (f32[80,128]{1,0:T(8,128)S(1)}, f32[80,128]{1,0:T(8,128)S(1)}, u32[]{:S(2)}, u32[]{:S(2)}) collective-permute-start(f32[80,128]{1,0:T(8,128)S(1)} %add_add_fusion.one_ref), channel_id=1, source_target_pairs={{0,1},{1,0},{2,3},{3,2},{4,5},{5,4},{6,7},{7,6},{8,9},{9,8},{10,11... | collective-permute-start | bytes 122888 | tf_op jit(solution)/shard_map/ppermute | solution.py:557
  148.3 2.7 %collective-permute-done.9.other_ref = f32[80,128]{1,0:T(8,128)S(1)} collective-permute-done((f32[80,128]{1,0:T(8,128)S(1)}, f32[80,128]{1,0:T(8,128)S(1)}, u32[]{:S(2)}, u32[]{:S(2)}) %collective-permute-start.9) | collective-permute-done | bytes 40992 | tf_op jit(solution)/shard_map/ppermute | solution.py:557
  151.0 0.9 shard_map.84
  (5 shorter events, 0.1 us)
Async XLA Ops:
  4.4 11.2 %copy-start.2 = (s32[16]{0:T(128)S(1)}, s32[16]{0:T(128)}, u32[]{:S(2)}) copy-start(s32[16]{0:T(128)} %param.9) | copy-start | bytes 196
  4.4 40.3 %all-to-all-start = ((f32[128,32,128]{2,1,0:T(8,128)}), f32[128,32,128]{2,1,0:T(8,128)S(1)}, u32[]{:S(2)}, u32[]{:S(2)}) async-start(f32[128,32,128]{2,1,0:T(8,128)} %shard_map.76), calls=%async_computation | async-start | bytes 4194304 | tf_op jit(solution)/shard_map/all_to_all | solution.py:625
  15.8 3.9 %copy-start = (f32[2,2,16,32,32]{4,3,2,1,0:T(8,128)S(1)}, f32[2,2,16,32,32]{4,3,2,1,0:T(8,128)}, u32[]{:S(2)}) copy-start(f32[2,2,16,32,32]{4,3,2,1,0:T(8,128)} %w_ref.1) | copy-start | bytes 786436
  15.8 3.9 %copy-start.1 = (f32[2,3,32,32]{3,2,1,0:T(8,128)S(1)}, f32[2,3,32,32]{3,2,1,0:T(8,128)}, u32[]{:S(2)}) copy-start(f32[2,3,32,32]{3,2,1,0:T(8,128)} %k_ref.1) | copy-start | bytes 73732
  44.7 34.5 %all-to-all-start.1 = ((f32[128,32,128]{2,1,0:T(8,128)}), f32[128,32,128]{2,1,0:T(8,128)}, u32[]{:S(2)}, u32[]{:S(2)}) async-start(f32[128,32,128]{2,1,0:T(8,128)} %shard_map.77), calls=%async_computation.1 | async-start | bytes 4194304 | tf_op jit(solution)/shard_map/all_to_all | solution.py:630
  95.4 37.4 %all-to-all-start.2 = ((f32[128,32,128]{2,1,0:T(8,128)}), f32[128,32,128]{2,1,0:T(8,128)S(1)}, u32[]{:S(2)}, u32[]{:S(2)}) async-start(f32[128,32,128]{2,1,0:T(8,128)} %bitcast.11), calls=%async_computation.2 | async-start | bytes 4194304 | tf_op jit(solution)/shard_map/all_to_all | solution.py:638
  110.5 17.3 %collective-permute-start = (f32[176,128]{1,0:T(8,128)S(1)}, f32[176,128]{1,0:T(8,128)S(1)}, u32[]{:S(2)}, u32[]{:S(2)}) collective-permute-start(f32[176,128]{1,0:T(8,128)S(1)} %get-tuple-element.93), channel_id=1, source_target_pairs={{0,32},{8,40},{16,48},{24,56},{32,64},{40,72},{48,80},{56,88},{64,... | collective-permute-start | bytes 270344 | tf_op jit(solution)/shard_map/ppermute | solution.py:557
  111.5 18.3 %collective-permute-start.1 = (f32[176,128]{1,0:T(8,128)S(1)}, f32[176,128]{1,0:T(8,128)S(1)}, u32[]{:S(2)}, u32[]{:S(2)}) collective-permute-start(f32[176,128]{1,0:T(8,128)S(1)} %get-tuple-element.94), channel_id=1, source_target_pairs={{0,64},{8,72},{16,80},{24,88},{32,96},{40,104},{48,112},{56,120},{... | collective-permute-start | bytes 270344 | tf_op jit(solution)/shard_map/ppermute | solution.py:557
  114.2 15.6 %collective-permute-start.2 = (f32[176,128]{1,0:T(8,128)S(1)}, f32[176,128]{1,0:T(8,128)S(1)}, u32[]{:S(2)}, u32[]{:S(2)}) collective-permute-start(f32[176,128]{1,0:T(8,128)S(1)} %get-tuple-element.95), channel_id=1, source_target_pairs={{0,96},{8,104},{16,112},{24,120},{32,0},{40,8},{48,16},{56,24},{64... | collective-permute-start | bytes 270344 | tf_op jit(solution)/shard_map/ppermute | solution.py:557
  129.9 6.7 %collective-permute-start.3 = (f32[80,128]{1,0:T(8,128)S(1)}, f32[80,128]{1,0:T(8,128)S(1)}, u32[]{:S(2)}, u32[]{:S(2)}) collective-permute-start(f32[80,128]{1,0:T(8,128)S(1)} %get-tuple-element.97), channel_id=1, source_target_pairs={{0,8},{8,16},{16,24},{24,0},{32,40},{40,48},{48,56},{56,32},{64,72... | collective-permute-start | bytes 122888 | tf_op jit(solution)/shard_map/ppermute | solution.py:557
  129.9 6.7 %collective-permute-start.4 = (f32[80,128]{1,0:T(8,128)S(1)}, f32[80,128]{1,0:T(8,128)S(1)}, u32[]{:S(2)}, u32[]{:S(2)}) collective-permute-start(f32[80,128]{1,0:T(8,128)S(1)} %get-tuple-element.98), channel_id=1, source_target_pairs={{0,16},{8,24},{16,0},{24,8},{32,48},{40,56},{48,32},{56,40},{64,80... | collective-permute-start | bytes 122888 | tf_op jit(solution)/shard_map/ppermute | solution.py:557
  131.5 5.1 %collective-permute-start.5 = (f32[80,128]{1,0:T(8,128)S(1)}, f32[80,128]{1,0:T(8,128)S(1)}, u32[]{:S(2)}, u32[]{:S(2)}) collective-permute-start(f32[80,128]{1,0:T(8,128)S(1)} %get-tuple-element.99), channel_id=1, source_target_pairs={{0,24},{8,0},{16,8},{24,16},{32,56},{40,32},{48,40},{56,48},{64,88... | collective-permute-start | bytes 122888 | tf_op jit(solution)/shard_map/ppermute | solution.py:557
  136.6 6.8 %collective-permute-start.6 = (f32[80,128]{1,0:T(8,128)S(1)}, f32[80,128]{1,0:T(8,128)S(1)}, u32[]{:S(2)}, u32[]{:S(2)}) collective-permute-start(f32[80,128]{1,0:T(8,128)S(1)} %add_add_fusion.1), channel_id=1, source_target_pairs={{0,4},{1,5},{2,6},{3,7},{4,0},{5,1},{6,2},{7,3},{8,12},{9,13},{10,... | collective-permute-start | bytes 122888 | tf_op jit(solution)/shard_map/ppermute | solution.py:557
  140.2 5.2 %collective-permute-start.7 = (f32[80,128]{1,0:T(8,128)S(1)}, f32[80,128]{1,0:T(8,128)S(1)}, u32[]{:S(2)}, u32[]{:S(2)}) collective-permute-start(f32[80,128]{1,0:T(8,128)S(1)} %add_add_fusion.1), channel_id=1, source_target_pairs={{0,2},{1,3},{2,4},{3,5},{4,6},{5,7},{6,0},{7,1},{8,10},{9,11},{10,... | collective-permute-start | bytes 122888 | tf_op jit(solution)/shard_map/ppermute | solution.py:557
  141.0 4.4 %collective-permute-start.8 = (f32[80,128]{1,0:T(8,128)S(1)}, f32[80,128]{1,0:T(8,128)S(1)}, u32[]{:S(2)}, u32[]{:S(2)}) collective-permute-start(f32[80,128]{1,0:T(8,128)S(1)} %add_add_fusion.1), channel_id=1, source_target_pairs={{0,6},{1,7},{2,0},{3,1},{4,2},{5,3},{6,4},{7,5},{8,14},{9,15},{10,... | collective-permute-start | bytes 122888 | tf_op jit(solution)/shard_map/ppermute | solution.py:557
  145.4 5.6 %collective-permute-start.9 = (f32[80,128]{1,0:T(8,128)S(1)}, f32[80,128]{1,0:T(8,128)S(1)}, u32[]{:S(2)}, u32[]{:S(2)}) collective-permute-start(f32[80,128]{1,0:T(8,128)S(1)} %add_add_fusion.one_ref), channel_id=1, source_target_pairs={{0,1},{1,0},{2,3},{3,2},{4,5},{5,4},{6,7},{7,6},{8,9},{9,8},{10,11... | collective-permute-start | bytes 122888 | tf_op jit(solution)/shard_map/ppermute | solution.py:557
where the time goes:
time: 152 us
  Pallas kernels  59 us (39%)
  waiting for transfers between devices  51.5 us (34%)
  starting transfers between devices  40.2 us (26%)
    ppermute x10, waiting for transfers between devices, shifted(): got.append(lax.ppermute(pieces[r], axis, perm))  18.9 us
    ppermute x10, starting transfers between devices, shifted(): got.append(lax.ppermute(pieces[r], axis, perm))  17.8 us
    all_to_all x1, waiting for transfers between devices, on_device(): cot_received = exchange(cot_blocks, everyone)  16.3 us
    all_to_all x1, waiting for transfers between devices, on_device(): received = exchange(to_blocks(input_field), everyone)  16.3 us
    pallas_call x1, Pallas kernels, backward(): pl.pallas_call(backward_kernel, in_specs=[ANY] + [HBM] * 9, out_specs=[HB...  16.1 us
    pallas_call x1, Pallas kernels, forward(): pl.pallas_call(forward_kernel, in_specs=[VMEM] * 8, out_specs=[VMEM] * 8,...  12.2 us
    all_to_all x1, starting transfers between devices, on_device(): received = exchange(to_blocks(input_field), everyone)  11.1 us
    pallas_call x1, Pallas kernels, weight_gradients(): pl.pallas_call(functools.partial(weight_kernel, scale), in_specs=[pl.Bloc...  9.69 us
  transfers between devices with their start and end apart: 13, of which 6 were waited for; matrix products, arithmetic and copies ran while one was open for 0% of the time, Pallas kernels for 25%

commit v1 on v0

--- a/solution.py
+++ b/solution.py
@@ -38,27 +38,37 @@
     return lax.dot_general(a, b, (dims, ((), ())), preferred_element_type=F32)
 
 
+FETCHED = 1
+SENT = 4
+
+
 def scatter_kernel(field_any, out_any, field, out, load_sem, store_sem):
-    steps, _, _, columns = field.shape
+    _, steps, _, columns = field.shape
     groups = LANES // J
-    loads = [
-        pltpu.make_async_copy(field_any.at[t], field.at[t], load_sem.at[t]) for t in range(steps)
-    ]
-    for copy in loads:
-        copy.start()
+    loads = []
+    for x in range(XB):
+        loads.append(
+            pltpu.make_async_copy(field_any.at[:, :, x, :], field.at[x], load_sem.at[x])
+        )
+        loads[-1].start()
+    for load in loads:
+        load.wait()
     stores = []
-    for q in range(columns // LANES):
+    count = columns // LANES
+    for q in range(count):
         lanes = slice(q * LANES, (q + 1) * LANES)
-        part = pl.ds(q * groups, groups)
         for t in range(steps):
-            if q == 0:
-                loads[t].wait()
-            rows = jnp.concatenate([field[t, :, x, lanes] for x in range(XB)], axis=0)
-            out[part, t * J : (t + 1) * J] = rows.T.reshape(groups, J, LANES)
-        stores.append(pltpu.make_async_copy(out.at[part], out_any.at[part], store_sem.at[q]))
-        stores[-1].start()
-    for copy in stores:
-        copy.wait()
+            rows = jnp.concatenate([field[x, t, :, lanes] for x in range(XB)], axis=0)
+            rows = rows.T.reshape(groups, J, LANES)
+            out[q * groups : (q + 1) * groups, t * J : (t + 1) * J] = rows
+        if (q + 1) % (count // SENT) == 0:
+            size = groups * count // SENT
+            part = pl.ds((q + 1) * groups - size, size)
+            sem = store_sem.at[len(stores)]
+            stores.append(pltpu.make_async_copy(out.at[part], out_any.at[part], sem))
+            stores[-1].start()
+    for store in stores:
+        store.wait()
 
 
 def gather_kernel(blocks_any, out_any, blocks, out, load_sem, store_sem):
@@ -66,29 +76,27 @@
     groups = LANES // J
     count = columns // LANES
     loads = []
-    for q in range(count):
-        part = pl.ds(q * groups, groups)
-        loads.append(pltpu.make_async_copy(blocks_any.at[part], blocks.at[part], load_sem.at[q]))
+    for i in range(FETCHED):
+        part = pl.ds(i * groups * count // FETCHED, groups * count // FETCHED)
+        loads.append(pltpu.make_async_copy(blocks_any.at[part], blocks.at[part], load_sem.at[i]))
         loads[-1].start()
     stores = []
-    for q in range(count):
-        lanes = slice(q * LANES, (q + 1) * LANES)
-        loads[q].wait()
-        for t in range(steps):
+    for t in range(steps):
+        for q in range(count):
+            lanes = slice(q * LANES, (q + 1) * LANES)
+            if t == 0 and q % (count // FETCHED) == 0:
+                loads[q // (count // FETCHED)].wait()
             rows = blocks[q * groups : (q + 1) * groups, t * J : (t + 1) * J]
             rows = rows.reshape(LANES, LANES).T
             for x in range(XB):
                 out[t, :, x, lanes] = rows[x * C : (x + 1) * C]
-        if q % 2 == 1:
-            done = pl.ds((q - 1) * LANES, 2 * LANES)
-            stores.append(
-                pltpu.make_async_copy(
-                    out.at[:, :, :, done], out_any.at[:, :, :, done], store_sem.at[q // 2]
-                )
-            )
+        if (t + 1) % (steps // SENT) == 0:
+            part = pl.ds(t + 1 - steps // SENT, steps // SENT)
+            sem = store_sem.at[len(stores)]
+            stores.append(pltpu.make_async_copy(out.at[part], out_any.at[part], sem))
             stores[-1].start()
-    for copy in stores:
-        copy.wait()
+    for store in stores:
+        store.wait()
 
 
 def to_blocks(field):
@@ -100,10 +108,10 @@
         out_specs=HBM,
         out_shape=pltpu.HBM(shape, F32),
         scratch_shapes=[
-            pltpu.VMEM(field.shape, F32),
+            pltpu.VMEM((XB, steps, C, columns), F32),
             pltpu.VMEM(shape, F32),
-            pltpu.SemaphoreType.DMA((steps,)),
-            pltpu.SemaphoreType.DMA((columns // LANES,)),
+            pltpu.SemaphoreType.DMA((XB,)),
+            pltpu.SemaphoreType.DMA((SENT,)),
         ],
         compiler_params=PARAMS,
     )(*in_hbm(field))
@@ -112,7 +120,6 @@
 def from_blocks(blocks):
     parts, rows, _ = blocks.shape
     shape = (rows // J, C, XB, parts * J)
-    count = shape[3] // LANES
     return pl.pallas_call(
         gather_kernel,
         in_specs=[ANY],
@@ -121,8 +128,8 @@
         scratch_shapes=[
             pltpu.VMEM(blocks.shape, F32),
             pltpu.VMEM(shape, F32),
-            pltpu.SemaphoreType.DMA((count,)),
-            pltpu.SemaphoreType.DMA((count // 2,)),
+            pltpu.SemaphoreType.DMA((FETCHED,)),
+            pltpu.SemaphoreType.DMA((SENT,)),
         ],
         compiler_params=PARAMS,
     )(blocks)
@@ -170,16 +177,16 @@
     return jnp.concatenate([own[0], own[0], own[1], both[0], edge[1]], axis=0)
 
 
-def prepare_kernel(scale, tab_ref, tabt_ref, w_ref, k_ref, ah, al, sh, sl, wh, wl, vh, vl, fb, bb):
-    ah[...], al[...] = widened(tab_ref[...])
-    sh[...], sl[...] = widened(tabt_ref[...])
+def prepare_kernel(scale, tab_ref, tabt_ref, w_ref, k_ref, at, st, wt, vt, fb, bb):
+    at[0], at[1] = widened(tab_ref[...])
+    st[0], st[1] = widened(tabt_ref[...])
     for l in range(w_ref.shape[0]):
 
         def body(m, _):
             re, im = w_ref[l, 0, m] * scale, w_ref[l, 1, m] * scale
-            wh[l, m], wl[l, m] = split(jnp.concatenate([re] * XB + [im] * XB, axis=1))
+            wt[0, l, m], wt[1, l, m] = split(jnp.concatenate([re] * XB + [im] * XB, axis=1))
             re, im = re.T, -im.T
-            vh[l, m], vl[l, m] = split(jnp.concatenate([re] * XB + [im] * XB, axis=1))
+            vt[0, l, m], vt[1, l, m] = split(jnp.concatenate([re] * XB + [im] * XB, axis=1))
             return 0
 
         lax.fori_loop(0, w_ref.shape[2], body, 0)
@@ -192,12 +199,12 @@
     layers, _, modes, channels, _ = spectral_weights.shape
     tab = angles(mode_list, total_time)
     rows, cols = 2 * modes * J, total_time * J
-    shapes = [(rows, cols)] * 2 + [(cols, rows)] * 2
-    shapes += [(layers, modes, channels, 2 * LANES)] * 4 + [(layers, 8 * LANES, 2 * LANES)] * 2
+    shapes = [(2, rows, cols), (2, cols, rows)]
+    shapes += [(2, layers, modes, channels, 2 * LANES)] * 2 + [(layers, 8 * LANES, 2 * LANES)] * 2
     return pl.pallas_call(
         functools.partial(prepare_kernel, scale),
         in_specs=[VMEM] * 4,
-        out_specs=[VMEM] * 10,
+        out_specs=[VMEM] * 6,
         out_shape=[pltpu.HBM(shape, BF16) for shape in shapes],
         compiler_params=PARAMS,
     )(tab, tab.T, spectral_weights, conv_kernel)
@@ -254,25 +261,25 @@
         analyse_pair(table, high_ref, low_ref, coef_ref, s)
 
 
-def mixing_matrix(w_ref, l, m):
+def mixing_matrix(w_ref, piece, l, m):
     row = lax.broadcasted_iota(jnp.int32, (LANES, 2 * LANES), 0) // C
     col = lax.broadcasted_iota(jnp.int32, (LANES, 2 * LANES), 1) // C % XB
-    wide = jnp.concatenate([w_ref[l, m]] * XB, axis=0)
+    wide = jnp.concatenate([w_ref[piece, l, m]] * XB, axis=0)
     top = jnp.where(row == col, wide, jnp.zeros_like(wide))
     return jnp.concatenate(
         [top, jnp.concatenate([-top[:, LANES:], top[:, :LANES]], axis=1)], axis=0
     )
 
 
-def mix(coef_ref, wh_ref, wl_ref, l, mixed_ref):
+def mix(coef_ref, w_ref, l, mixed_ref):
     bricks = coef_ref.shape[0]
-    for m in range(wh_ref.shape[1]):
+    for m in range(w_ref.shape[2]):
         re, im = slice(2 * J * m, 2 * J * m + J), slice(2 * J * m + J, 2 * J * (m + 1))
         value = jnp.concatenate(
             [coef_ref[:, re].reshape(bricks * J, LANES), coef_ref[:, im].reshape(bricks * J, LANES)],
             axis=1,
         )
-        matrix = (mixing_matrix(wh_ref, l, m), mixing_matrix(wl_ref, l, m))
+        matrix = tuple(mixing_matrix(w_ref, piece, l, m) for piece in range(2))
         result = dot3(split(value), matrix)
         mixed_ref[:, re] = result[:, :LANES].reshape(bricks, J, LANES)
         mixed_ref[:, im] = result[:, LANES:].reshape(bricks, J, LANES)
@@ -299,13 +306,13 @@
 
 
 def forward_kernel(
-    x_ref, ah, al, sh, sl, wh, wl, fb,
+    x_ref, at, st, wt, fb,
     coef1, coef2, slope1, slope2, x1h, x1l, x2h, x2l, mixed,
 ):
     bricks = x_ref.shape[1]
     for s in range(bricks):
         put_split(brick(x_ref, s), s, x1h, x1l)
-    analysis, synthesis = (ah[...], al[...]), (sh[...], sl[...])
+    analysis, synthesis = (at[0], at[1]), (st[0], st[1])
 
     def first(s, z):
         value, slope = gelu_parts(z)
@@ -319,58 +326,48 @@
         ((x1h, x1l, coef1, first), (x2h, x2l, coef2, second))
     ):
         analyse(analysis, h, low, coef)
-        mix(coef, wh, wl, l, mixed)
+        mix(coef, wt, l, mixed)
         synthesise(synthesis, mixed, fb[l], h, low, emit)
 
 
-def forward(field, tabs, weights, bands_):
+def forward(field, *tables):
     _, bricks, _, _ = field.shape
-    rows = tabs[0].shape[1]
-    modes = tabs[0].shape[0]
+    _, modes, rows = tables[0].shape
     coef = pltpu.HBM((bricks, modes, LANES), F32)
     full = pltpu.HBM((bricks, rows, LANES), F32)
     half = pltpu.HBM((bricks, rows, LANES), BF16)
     return pl.pallas_call(
         forward_kernel,
-        in_specs=[VMEM] * 8,
+        in_specs=[VMEM] * 5,
         out_specs=[VMEM] * 8,
         out_shape=[coef, coef, full, full, half, half, half, half],
         scratch_shapes=[pltpu.VMEM((bricks, modes, LANES), F32)],
         compiler_params=PARAMS,
-    )(field, *in_hbm(*tabs, *weights, *bands_))
+    )(field, *in_hbm(*tables))
 
 
 def backward_kernel(*refs):
     g_any, slope1_any, slope2_any = refs[:3]
-    small_any = refs[3:10]
-    out_any, sens1_any, sens2_any = refs[10:13]
-    z_any = refs[13:17]
-    g, slope1, slope2 = refs[17:20]
-    small = refs[20:27]
-    sens1, sens2, z1h, z1l, z2h, z2l, out, mixed, load_sem, small_sem, store_sem = refs[27:]
-    ah, al, sh, sl, wh, wl, bb = small
-    bricks = g.shape[0]
+    small_any = refs[3:7]
+    out_any, sens1_any, sens2_any = refs[7:10]
+    z_any = refs[10:14]
+    g, slope1, slope2 = refs[14:17]
+    small = refs[17:21]
+    sens1, sens2, z1h, z1l, z2h, z2l, out, mixed, load_sem, small_sem, store_sem = refs[21:]
+    at, st, wt, bb = small
+    bricks = slope1.shape[0]
     copy = pltpu.make_async_copy
 
-    loads = [
-        (
-            copy(g_any.at[:, s], g.at[s], load_sem.at[0, s]),
-            copy(slope2_any.at[s], slope2.at[s], load_sem.at[1, s]),
-            copy(slope1_any.at[s], slope1.at[s], load_sem.at[2, s]),
-        )
-        for s in range(bricks)
-    ]
+    half = bricks // 2
+    loads = []
+    for i, part in enumerate((pl.ds(0, half), pl.ds(half, half))):
+        loads.append(copy(g_any.at[:, part], g.at[:, part], load_sem.at[2 * i]))
+        loads.append(copy(slope2_any.at[part], slope2.at[part], load_sem.at[2 * i + 1]))
+    loads.append(copy(slope1_any, slope1, load_sem.at[4]))
     tables = [copy(a, r, small_sem.at[i]) for i, (a, r) in enumerate(zip(small_any, small))]
-    for s in range(bricks):
-        loads[s][0].start()
-        loads[s][1].start()
-        if s == 1:
-            tables[0].start()
-            tables[1].start()
-    for i in (4, 5, 2, 3, 6):
-        tables[i].start()
-    for s in range(bricks):
-        loads[s][2].start()
+    tables[0].start()
+    for load in loads[:4]:
+        load.start()
 
     stores = []
 
@@ -378,64 +375,71 @@
         stores.append(copy(source, target, store_sem.at[len(stores)]))
         stores[-1].start()
 
+    for load in (tables[0], loads[0], loads[1]):
+        load.wait()
+    for load in (tables[2], tables[1], tables[3], loads[4]):
+        load.start()
+    analysis = (at[0], at[1])
     for s in range(0, bricks, 2):
+        if s == half:
+            for load in loads[2:4]:
+                load.wait()
         for o in (s, s + 1):
-            loads[o][0].wait()
-            loads[o][1].wait()
-        if s == 0:
-            tables[0].wait()
-            tables[1].wait()
-        for o in (s, s + 1):
-            put_split(g[o].reshape(-1, LANES) * slope2[o], o, z2h, z2l)
-        analyse_pair((ah[...], al[...]), z2h, z2l, sens2, s)
+            put_split(brick(g, o) * slope2[o], o, z2h, z2l)
+        analyse_pair(analysis, z2h, z2l, sens2, s)
     store(z2h, z_any[2])
     store(z2l, z_any[3])
     store(sens2, sens2_any)
-    for i in range(2, 7):
-        tables[i].wait()
-    analysis, synthesis = (ah[...], al[...]), (sh[...], sl[...])
+    tables[2].wait()
+    mix(sens2, wt, 1, mixed)
+    tables[1].wait()
+    tables[3].wait()
+    synthesis = (st[0], st[1])
 
     def second(s, value):
-        loads[s][2].wait()
+        if s == 0:
+            loads[4].wait()
         put_split(value * slope1[s], s, z1h, z1l)
 
     def first(s, value):
-        out[s] = value.reshape(out.shape[1:])
-        store(out.at[s], out_any.at[:, s])
-
-    mix(sens2, wh, wl, 1, mixed)
+        out[:, s] = value.reshape(out.shape[0], -1, LANES)
+        if s % STORED == STORED - 1:
+            done = pl.ds(s - STORED + 1, STORED)
+            store(out.at[:, done], out_any.at[:, done])
+
     synthesise(synthesis, mixed, bb[1], z2h, z2l, second)
     store(z1h, z_any[0])
     store(z1l, z_any[1])
     analyse(analysis, z1h, z1l, sens1)
     store(sens1, sens1_any)
-    mix(sens1, wh, wl, 0, mixed)
+    mix(sens1, wt, 0, mixed)
     synthesise(synthesis, mixed, bb[0], z1h, z1l, first)
     for done in stores:
         done.wait()
 
 
-def backward(cotangent, slope1, slope2, tabs, weights, bands_):
+STORED = 4
+
+
+def backward(cotangent, slope1, slope2, *tables):
     groups, bricks, lines, _ = cotangent.shape
-    rows = tabs[0].shape[1]
-    modes = tabs[0].shape[0]
+    _, modes, rows = tables[0].shape
     coef = ((bricks, modes, LANES), F32)
     half = ((bricks, rows, LANES), BF16)
-    brick_shape = ((bricks, groups, lines, LANES), F32)
     outs = [(cotangent.shape, F32), coef, coef, half, half, half, half]
-    operands = (cotangent, slope1, slope2, *tabs, *weights, *bands_)
-    scratch = [brick_shape] + [(o.shape, o.dtype) for o in operands[1:]]
-    scratch += [coef, coef, half, half, half, half, brick_shape, coef]
+    operands = (cotangent, slope1, slope2, *tables)
+    scratch = [(o.shape, o.dtype) for o in operands]
+    scratch += [coef, coef, half, half, half, half, (cotangent.shape, F32), coef]
     return pl.pallas_call(
         backward_kernel,
-        in_specs=[ANY] + [HBM] * 9,
+        in_specs=[ANY] + [HBM] * 6,
         out_specs=[HBM] * 7,
         out_shape=[pltpu.HBM(*o) for o in outs],
         scratch_shapes=[pltpu.VMEM(*o) for o in scratch]
         + [
-            pltpu.SemaphoreType.DMA((3, bricks)),
-            pltpu.SemaphoreType.DMA((7,)),
-            pltpu.SemaphoreType.DMA((6 + bricks,)),
+            pltpu.SemaphoreType.DMA((5,)),
+            pltpu.SemaphoreType.DMA((4,)),
+            pltpu.SemaphoreType.DMA((6 + bricks // STORED,)),
         ],
         compiler_params=PARAMS,
     )(cotangent, *in_hbm(*operands[1:]))
@@ -626,14 +630,20 @@
     cot_blocks = to_blocks(cotangent)
     prepared = prepare(scale, spectral_weights, conv_kernel, mode_list, total_time)
     received, cot_blocks, prepared = lax.optimization_barrier((received, cot_blocks, prepared))
-    tabs = prepared[:4]
+    analysis, synthesis, mix_forward, mix_backward, band_forward, band_backward = prepared
     cot_received = exchange(cot_blocks, everyone)
     shape = (groups, bricks, steps * J, LANES)
     coef1, coef2, slope1, slope2, x1h, x1l, x2h, x2l = forward(
-        received.reshape(shape), tabs, prepared[4:6], prepared[8:9]
+        received.reshape(shape), analysis, synthesis, mix_forward, band_forward
     )
     grad, sens1, sens2, z1h, z1l, z2h, z2l = backward(
-        cot_received.reshape(shape), slope1, slope2, tabs, prepared[6:8], prepared[9:]
+        cot_received.reshape(shape),
+        slope1,
+        slope2,
+        analysis,
+        synthesis,
+        mix_backward,
+        band_backward,
     )
     returned = exchange(grad.reshape(cot_received.shape), everyone)
     me = lax.axis_index("tm").astype(jnp.int32)

time: 152 us -> 147 us (0.967)
  Pallas kernels: 59 us -> 53.4 us
    pallas_call x2, Pallas kernels: 28.4 us -> 25.2 us  [the longest x1 13.1 us: backward(): pl.pallas_call(backward_kernel, in_specs=[ANY] + [HBM] * 6, out_specs=[HB...]
where the time goes in v1:
time: 147 us
  Pallas kernels  53.4 us (36%)
  waiting for transfers between devices  52.2 us (36%)
  starting transfers between devices  40.2 us (27%)
    ppermute x10, waiting for transfers between devices, shifted(): got.append(lax.ppermute(pieces[r], axis, perm))  18.9 us
    ppermute x10, starting transfers between devices, shifted(): got.append(lax.ppermute(pieces[r], axis, perm))  17.8 us
    all_to_all x1, waiting for transfers between devices, on_device(): received = exchange(to_blocks(input_field), everyone)  16.9 us
    all_to_all x1, waiting for transfers between devices, on_device(): cot_received = exchange(cot_blocks, everyone)  16.4 us
    pallas_call x1, Pallas kernels, backward(): pl.pallas_call(backward_kernel, in_specs=[ANY] + [HBM] * 6, out_specs=[HB...  13.1 us
    pallas_call x1, Pallas kernels, forward(): pl.pallas_call(forward_kernel, in_specs=[VMEM] * 5, out_specs=[VMEM] * 8,...  12.1 us
    all_to_all x1, starting transfers between devices, on_device(): received = exchange(to_blocks(input_field), everyone)  11.1 us
    pallas_call x1, Pallas kernels, weight_gradients(): pl.pallas_call(functools.partial(weight_kernel, scale), in_specs=[pl.Bloc...  9.69 us
  transfers between devices with their start and end apart: 13, of which 6 were waited for; matrix products, arithmetic and copies ran while one was open for 0% of the time, Pallas kernels for 25%

profile of v1, /device:TPU:0, one launch (start us, length us, event | category | flops | bytes accessed | tf_op | source)
XLA Modules:
  0.0 146.9 jit_solution(991239830772291416)
XLA Ops:
  0.6 3.2 %shard_map.76 = f32[128,32,128]{2,1,0:T(8,128)} custom-call(f32[4,32,4,1024]{3,2,1,0:T(4,128)} %field_any.2), custom_call_target="tpu_custom_call" | custom-call | tf_op jit(solution)/shard_map/pallas_call | solution.py:105
  3.8 0.0 copy-start.2
  3.9 11.1 %all-to-all-start = ((f32[128,32,128]{2,1,0:T(8,128)}), f32[128,32,128]{2,1,0:T(8,128)S(1)}, u32[]{:S(2)}, u32[]{:S(2)}) async-start(f32[128,32,128]{2,1,0:T(8,128)} %shard_map.76), calls=%async_computation | async-start | bytes 4194304 | tf_op jit(solution)/shard_map/all_to_all | solution.py:629
  15.0 0.0 copy-done.2
  15.0 0.1 fusion.6
  15.2 0.1 copy.11
  15.3 0.0 copy-start
  15.3 0.0 copy-start.1
  15.3 3.3 %shard_map.77 = f32[128,32,128]{2,1,0:T(8,128)} custom-call(f32[4,32,4,1024]{3,2,1,0:T(4,128)} %field_any.3), custom_call_target="tpu_custom_call" | custom-call | tf_op jit(solution)/shard_map/pallas_call | solution.py:105
  18.6 0.0 copy-done
  18.6 0.0 copy-done.1
  18.6 8.7 %shard_map.78 = (bf16[2,256,512]{2,1,0:T(8,128)(2,1)}, bf16[2,512,256]{2,1,0:T(8,128)(2,1)}, bf16[2,2,16,32,256]{4,3,2,1,0:T(8,128)(2,1)}, bf16[2,2,16,32,256]{4...) custom-call(f32[32,64]{1,0:T(8,128)S(1)} %bitcast.9, f32[64,32]{1,0:T(8,128)S(1)} %bitcast.10, ...), custom_call_target="tpu_custom_call" | custom-call | tf_op jit(solution)/shard_map/pallas_call | solution.py:204
  27.3 16.9 %all-to-all-done = f32[128,32,128]{2,1,0:T(8,128)S(1)} async-done(((f32[128,32,128]{2,1,0:T(8,128)}), f32[128,32,128]{2,1,0:T(8,128)S(1)}, u32[]{:S(2)}, u32[]{:S(2)}) %all-to-all-start) | async-done | bytes 2097184 | tf_op jit(solution)/shard_map/all_to_all | solution.py:629
  44.2 6.0 %all-to-all-start.1 = ((f32[128,32,128]{2,1,0:T(8,128)}), f32[128,32,128]{2,1,0:T(8,128)}, u32[]{:S(2)}, u32[]{:S(2)}) async-start(f32[128,32,128]{2,1,0:T(8,128)} %shard_map.77), calls=%async_computation.1 | async-start | bytes 4194304 | tf_op jit(solution)/shard_map/all_to_all | solution.py:634
  50.2 12.1 %shard_map.79 = (f32[8,256,128]{2,1,0:T(8,128)}, f32[8,256,128]{2,1,0:T(8,128)}, f32[8,512,128]{2,1,0:T(8,128)}, f32[8,512,128]{2,1,0:T(8,128)}, bf16[8,512,128]...) custom-call(f32[16,8,32,128]{3,2,1,0:T(8,128)S(1)} %bitcast.7, ...), custom_call_target="tpu_custom_call" | custom-call | tf_op jit(solution)/shard_map/pallas_call | solution.py:339
  62.3 16.4 %all-to-all-done.1 = f32[128,32,128]{2,1,0:T(8,128)} async-done(((f32[128,32,128]{2,1,0:T(8,128)}), f32[128,32,128]{2,1,0:T(8,128)}, u32[]{:S(2)}, u32[]{:S(2)}) %all-to-all-start.1) | async-done | bytes 2097184 | tf_op jit(solution)/shard_map/all_to_all | solution.py:634
  78.7 13.1 %shard_map.80 = (f32[16,8,32,128]{3,2,1,0:T(8,128)}, f32[8,256,128]{2,1,0:T(8,128)}, f32[8,256,128]{2,1,0:T(8,128)}, bf16[8,512,128]{2,1,0:T(8,128)(2,1)}, bf16[...) custom-call(f32[16,8,32,128]{3,2,1,0:T(8,128)} %bitcast.2.refs_0_, ...), custom_call_target="tpu_custom_call" | custom-call | tf_op jit(solution)/shard_map/pallas_call | solution.py:433
  91.8 5.3 %all-to-all-start.2 = ((f32[128,32,128]{2,1,0:T(8,128)}), f32[128,32,128]{2,1,0:T(8,128)S(1)}, u32[]{:S(2)}, u32[]{:S(2)}) async-start(f32[128,32,128]{2,1,0:T(8,128)} %bitcast.11), calls=%async_computation.2 | async-start | bytes 4194304 | tf_op jit(solution)/shard_map/all_to_all | solution.py:648
  97.1 0.1 pad_add_fusion.me_ref
  97.2 9.7 %shard_map.82 = (f32[176,128]{1,0:T(8,128)S(1)}, f32[176,128]{1,0:T(8,128)S(1)}, f32[176,128]{1,0:T(8,128)S(1)}, f32[176,128]{1,0:T(8,128)S(1)}) custom-call(s32[2]{0:T(128)S(1)} %pad_add_fusion.me_ref, f32[8,256,128]{2,1,0:T(8,128)} %get-tuple-element.64.refs_0_, f32[8,256,128]{2,1,0:T(8,128)} %get-tuple-element.65.refs_1_, ...), custom_call_target="tpu_custom_call" | custom-call | tf_op jit(solution)/shard_map/pallas_call | solution.py:538
  106.9 1.0 collective-permute-start
  107.9 2.7 %collective-permute-start.1 = (f32[176,128]{1,0:T(8,128)S(1)}, f32[176,128]{1,0:T(8,128)S(1)}, u32[]{:S(2)}, u32[]{:S(2)}) collective-permute-start(f32[176,128]{1,0:T(8,128)S(1)} %get-tuple-element.78), channel_id=1, source_target_pairs={{0,64},{8,72},{16,80},{24,88},{32,96},{40,104},{48,112},{56,120},{... | collective-permute-start | bytes 270344 | tf_op jit(solution)/shard_map/ppermute | solution.py:561
  110.6 1.5 collective-permute-start.2
  112.1 12.1 %collective-permute-done.refs_1_ = f32[176,128]{1,0:T(8,128)S(1)} collective-permute-done((f32[176,128]{1,0:T(8,128)S(1)}, f32[176,128]{1,0:T(8,128)S(1)}, u32[]{:S(2)}, u32[]{:S(2)}) %collective-permute-start) | collective-permute-done | bytes 90144 | tf_op jit(solution)/shard_map/ppermute | solution.py:561
  124.2 2.0 %collective-permute-done.1.refs_2_ = f32[176,128]{1,0:T(8,128)S(1)} collective-permute-done((f32[176,128]{1,0:T(8,128)S(1)}, f32[176,128]{1,0:T(8,128)S(1)}, u32[]{:S(2)}, u32[]{:S(2)}) %collective-permute-start.1) | collective-permute-done | bytes 90144 | tf_op jit(solution)/shard_map/ppermute | solution.py:561
  126.3 0.0 collective-permute-done.2.refs_3_
  126.3 0.1 collective-permute-start.3
  126.4 1.5 %collective-permute-start.4 = (f32[80,128]{1,0:T(8,128)S(1)}, f32[80,128]{1,0:T(8,128)S(1)}, u32[]{:S(2)}, u32[]{:S(2)}) collective-permute-start(f32[80,128]{1,0:T(8,128)S(1)} %get-tuple-element.82), channel_id=1, source_target_pairs={{0,16},{8,24},{16,0},{24,8},{32,48},{40,56},{48,32},{56,40},{64,80... | collective-permute-start | bytes 122888 | tf_op jit(solution)/shard_map/ppermute | solution.py:561
  127.9 1.4 collective-permute-start.5
  129.3 0.0 all-to-all-done.2.blocks_any
  129.3 2.4 %shard_map.81 = f32[4,32,4,1024]{3,2,1,0:T(4,128)} custom-call(f32[128,32,128]{2,1,0:T(8,128)S(1)} %all-to-all-done.2.blocks_any), custom_call_target="tpu_custom_call" | custom-call | tf_op jit(solution)/shard_map/pallas_call | solution.py:123
  131.7 0.0 collective-permute-done.3
  131.7 0.0 collective-permute-done.4
  131.7 0.0 collective-permute-done.5
  131.7 3.5 %collective-permute-start.6 = (f32[80,128]{1,0:T(8,128)S(1)}, f32[80,128]{1,0:T(8,128)S(1)}, u32[]{:S(2)}, u32[]{:S(2)}) collective-permute-start(f32[80,128]{1,0:T(8,128)S(1)} %add_add_fusion.1), channel_id=1, source_target_pairs={{0,4},{1,5},{2,6},{3,7},{4,0},{5,1},{6,2},{7,3},{8,12},{9,13},{10,... | collective-permute-start | bytes 122888 | tf_op jit(solution)/shard_map/ppermute | solution.py:561
  135.2 0.8 collective-permute-start.7
  136.1 2.4 %collective-permute-start.8 = (f32[80,128]{1,0:T(8,128)S(1)}, f32[80,128]{1,0:T(8,128)S(1)}, u32[]{:S(2)}, u32[]{:S(2)}) collective-permute-start(f32[80,128]{1,0:T(8,128)S(1)} %add_add_fusion.1), channel_id=1, source_target_pairs={{0,6},{1,7},{2,0},{3,1},{4,2},{5,3},{6,4},{7,5},{8,14},{9,15},{10,... | collective-permute-start | bytes 122888 | tf_op jit(solution)/shard_map/ppermute | solution.py:561
  138.5 0.0 collective-permute-done.6
  138.5 2.0 %collective-permute-done.7 = f32[80,128]{1,0:T(8,128)S(1)} collective-permute-done((f32[80,128]{1,0:T(8,128)S(1)}, f32[80,128]{1,0:T(8,128)S(1)}, u32[]{:S(2)}, u32[]{:S(2)}) %collective-permute-start.7) | collective-permute-done | bytes 40992 | tf_op jit(solution)/shard_map/ppermute | solution.py:561
  140.5 0.0 collective-permute-done.8
  140.5 2.9 %collective-permute-start.9 = (f32[80,128]{1,0:T(8,128)S(1)}, f32[80,128]{1,0:T(8,128)S(1)}, u32[]{:S(2)}, u32[]{:S(2)}) collective-permute-start(f32[80,128]{1,0:T(8,128)S(1)} %add_add_fusion.one_ref), channel_id=1, source_target_pairs={{0,1},{1,0},{2,3},{3,2},{4,5},{5,4},{6,7},{7,6},{8,9},{9,8},{10,11... | collective-permute-start | bytes 122888 | tf_op jit(solution)/shard_map/ppermute | solution.py:561
  143.4 2.7 %collective-permute-done.9.other_ref = f32[80,128]{1,0:T(8,128)S(1)} collective-permute-done((f32[80,128]{1,0:T(8,128)S(1)}, f32[80,128]{1,0:T(8,128)S(1)}, u32[]{:S(2)}, u32[]{:S(2)}) %collective-permute-start.9) | collective-permute-done | bytes 40992 | tf_op jit(solution)/shard_map/ppermute | solution.py:561
  146.1 0.9 shard_map.84
  (5 shorter events, 0.1 us)
Async XLA Ops:
  3.8 11.2 %copy-start.2 = (s32[16]{0:T(128)S(1)}, s32[16]{0:T(128)}, u32[]{:S(2)}) copy-start(s32[16]{0:T(128)} %param.9) | copy-start | bytes 196
  3.9 40.3 %all-to-all-start = ((f32[128,32,128]{2,1,0:T(8,128)}), f32[128,32,128]{2,1,0:T(8,128)S(1)}, u32[]{:S(2)}, u32[]{:S(2)}) async-start(f32[128,32,128]{2,1,0:T(8,128)} %shard_map.76), calls=%async_computation | async-start | bytes 4194304 | tf_op jit(solution)/shard_map/all_to_all | solution.py:629
  15.3 3.3 %copy-start = (f32[2,2,16,32,32]{4,3,2,1,0:T(8,128)S(1)}, f32[2,2,16,32,32]{4,3,2,1,0:T(8,128)}, u32[]{:S(2)}) copy-start(f32[2,2,16,32,32]{4,3,2,1,0:T(8,128)} %w_ref.1) | copy-start | bytes 786436
  15.3 3.3 %copy-start.1 = (f32[2,3,32,32]{3,2,1,0:T(8,128)S(1)}, f32[2,3,32,32]{3,2,1,0:T(8,128)}, u32[]{:S(2)}) copy-start(f32[2,3,32,32]{3,2,1,0:T(8,128)} %k_ref.1) | copy-start | bytes 73732
  44.2 34.5 %all-to-all-start.1 = ((f32[128,32,128]{2,1,0:T(8,128)}), f32[128,32,128]{2,1,0:T(8,128)}, u32[]{:S(2)}, u32[]{:S(2)}) async-start(f32[128,32,128]{2,1,0:T(8,128)} %shard_map.77), calls=%async_computation.1 | async-start | bytes 4194304 | tf_op jit(solution)/shard_map/all_to_all | solution.py:634
  91.8 37.4 %all-to-all-start.2 = ((f32[128,32,128]{2,1,0:T(8,128)}), f32[128,32,128]{2,1,0:T(8,128)S(1)}, u32[]{:S(2)}, u32[]{:S(2)}) async-start(f32[128,32,128]{2,1,0:T(8,128)} %bitcast.11), calls=%async_computation.2 | async-start | bytes 4194304 | tf_op jit(solution)/shard_map/all_to_all | solution.py:648
  106.9 17.3 %collective-permute-start = (f32[176,128]{1,0:T(8,128)S(1)}, f32[176,128]{1,0:T(8,128)S(1)}, u32[]{:S(2)}, u32[]{:S(2)}) collective-permute-start(f32[176,128]{1,0:T(8,128)S(1)} %get-tuple-element.77), channel_id=1, source_target_pairs={{0,32},{8,40},{16,48},{24,56},{32,64},{40,72},{48,80},{56,88},{64,... | collective-permute-start | bytes 270344 | tf_op jit(solution)/shard_map/ppermute | solution.py:561
  107.9 18.3 %collective-permute-start.1 = (f32[176,128]{1,0:T(8,128)S(1)}, f32[176,128]{1,0:T(8,128)S(1)}, u32[]{:S(2)}, u32[]{:S(2)}) collective-permute-start(f32[176,128]{1,0:T(8,128)S(1)} %get-tuple-element.78), channel_id=1, source_target_pairs={{0,64},{8,72},{16,80},{24,88},{32,96},{40,104},{48,112},{56,120},{... | collective-permute-start | bytes 270344 | tf_op jit(solution)/shard_map/ppermute | solution.py:561
  110.6 15.6 %collective-permute-start.2 = (f32[176,128]{1,0:T(8,128)S(1)}, f32[176,128]{1,0:T(8,128)S(1)}, u32[]{:S(2)}, u32[]{:S(2)}) collective-permute-start(f32[176,128]{1,0:T(8,128)S(1)} %get-tuple-element.79), channel_id=1, source_target_pairs={{0,96},{8,104},{16,112},{24,120},{32,0},{40,8},{48,16},{56,24},{64... | collective-permute-start | bytes 270344 | tf_op jit(solution)/shard_map/ppermute | solution.py:561
  126.3 5.4 %collective-permute-start.3 = (f32[80,128]{1,0:T(8,128)S(1)}, f32[80,128]{1,0:T(8,128)S(1)}, u32[]{:S(2)}, u32[]{:S(2)}) collective-permute-start(f32[80,128]{1,0:T(8,128)S(1)} %get-tuple-element.81), channel_id=1, source_target_pairs={{0,8},{8,16},{16,24},{24,0},{32,40},{40,48},{48,56},{56,32},{64,72... | collective-permute-start | bytes 122888 | tf_op jit(solution)/shard_map/ppermute | solution.py:561
  126.4 5.3 %collective-permute-start.4 = (f32[80,128]{1,0:T(8,128)S(1)}, f32[80,128]{1,0:T(8,128)S(1)}, u32[]{:S(2)}, u32[]{:S(2)}) collective-permute-start(f32[80,128]{1,0:T(8,128)S(1)} %get-tuple-element.82), channel_id=1, source_target_pairs={{0,16},{8,24},{16,0},{24,8},{32,48},{40,56},{48,32},{56,40},{64,80... | collective-permute-start | bytes 122888 | tf_op jit(solution)/shard_map/ppermute | solution.py:561
  127.9 3.8 %collective-permute-start.5 = (f32[80,128]{1,0:T(8,128)S(1)}, f32[80,128]{1,0:T(8,128)S(1)}, u32[]{:S(2)}, u32[]{:S(2)}) collective-permute-start(f32[80,128]{1,0:T(8,128)S(1)} %get-tuple-element.83), channel_id=1, source_target_pairs={{0,24},{8,0},{16,8},{24,16},{32,56},{40,32},{48,40},{56,48},{64,88... | collective-permute-start | bytes 122888 | tf_op jit(solution)/shard_map/ppermute | solution.py:561
  131.7 6.8 %collective-permute-start.6 = (f32[80,128]{1,0:T(8,128)S(1)}, f32[80,128]{1,0:T(8,128)S(1)}, u32[]{:S(2)}, u32[]{:S(2)}) collective-permute-start(f32[80,128]{1,0:T(8,128)S(1)} %add_add_fusion.1), channel_id=1, source_target_pairs={{0,4},{1,5},{2,6},{3,7},{4,0},{5,1},{6,2},{7,3},{8,12},{9,13},{10,... | collective-permute-start | bytes 122888 | tf_op jit(solution)/shard_map/ppermute | solution.py:561
  135.2 5.2 %collective-permute-start.7 = (f32[80,128]{1,0:T(8,128)S(1)}, f32[80,128]{1,0:T(8,128)S(1)}, u32[]{:S(2)}, u32[]{:S(2)}) collective-permute-start(f32[80,128]{1,0:T(8,128)S(1)} %add_add_fusion.1), channel_id=1, source_target_pairs={{0,2},{1,3},{2,4},{3,5},{4,6},{5,7},{6,0},{7,1},{8,10},{9,11},{10,... | collective-permute-start | bytes 122888 | tf_op jit(solution)/shard_map/ppermute | solution.py:561
  136.1 4.4 %collective-permute-start.8 = (f32[80,128]{1,0:T(8,128)S(1)}, f32[80,128]{1,0:T(8,128)S(1)}, u32[]{:S(2)}, u32[]{:S(2)}) collective-permute-start(f32[80,128]{1,0:T(8,128)S(1)} %add_add_fusion.1), channel_id=1, source_target_pairs={{0,6},{1,7},{2,0},{3,1},{4,2},{5,3},{6,4},{7,5},{8,14},{9,15},{10,... | collective-permute-start | bytes 122888 | tf_op jit(solution)/shard_map/ppermute | solution.py:561
  140.5 5.6 %collective-permute-start.9 = (f32[80,128]{1,0:T(8,128)S(1)}, f32[80,128]{1,0:T(8,128)S(1)}, u32[]{:S(2)}, u32[]{:S(2)}) collective-permute-start(f32[80,128]{1,0:T(8,128)S(1)} %add_add_fusion.one_ref), channel_id=1, source_target_pairs={{0,1},{1,0},{2,3},{3,2},{4,5},{5,4},{6,7},{7,6},{8,9},{9,8},{10,11... | collective-permute-start | bytes 122888 | tf_op jit(solution)/shard_map/ppermute | solution.py:561

commit v2 on v1

--- a/solution.py
+++ b/solution.py
@@ -42,31 +42,36 @@
 SENT = 4
 
 
-def scatter_kernel(field_any, out_any, field, out, load_sem, store_sem):
-    _, steps, _, columns = field.shape
+def scatter_kernel(first_any, second_any, out_any, field, out, load_sem, store_sem):
+    _, _, steps, _, columns = field.shape
     groups = LANES // J
-    loads = []
-    for x in range(XB):
-        loads.append(
-            pltpu.make_async_copy(field_any.at[:, :, x, :], field.at[x], load_sem.at[x])
+    loads = [
+        pltpu.make_async_copy(
+            source.at[:, :, x, :], field.at[which, x], load_sem.at[which, x]
         )
-        loads[-1].start()
+        for which, source in enumerate((first_any, second_any))
+        for x in range(XB)
+    ]
     for load in loads:
-        load.wait()
+        load.start()
     stores = []
     count = columns // LANES
-    for q in range(count):
-        lanes = slice(q * LANES, (q + 1) * LANES)
-        for t in range(steps):
-            rows = jnp.concatenate([field[x, t, :, lanes] for x in range(XB)], axis=0)
-            rows = rows.T.reshape(groups, J, LANES)
-            out[q * groups : (q + 1) * groups, t * J : (t + 1) * J] = rows
-        if (q + 1) % (count // SENT) == 0:
-            size = groups * count // SENT
-            part = pl.ds((q + 1) * groups - size, size)
-            sem = store_sem.at[len(stores)]
-            stores.append(pltpu.make_async_copy(out.at[part], out_any.at[part], sem))
-            stores[-1].start()
+    for which in range(2):
+        for load in loads[which * XB : (which + 1) * XB]:
+            load.wait()
+        for q in range(count):
+            lanes = slice(q * LANES, (q + 1) * LANES)
+            for t in range(steps):
+                at = (which * steps + t) * J
+                rows = jnp.concatenate([field[which, x, t, :, lanes] for x in range(XB)], axis=0)
+                rows = rows.T.reshape(groups, J, LANES)
+                out[q * groups : (q + 1) * groups, at : at + J] = rows
+            if which == 1 and (q + 1) % (count // SENT) == 0:
+                size = groups * count // SENT
+                part = pl.ds((q + 1) * groups - size, size)
+                sem = store_sem.at[len(stores)]
+                stores.append(pltpu.make_async_copy(out.at[part], out_any.at[part], sem))
+                stores[-1].start()
     for store in stores:
         store.wait()
 
@@ -99,22 +104,22 @@
         store.wait()
 
 
-def to_blocks(field):
-    steps, _, _, columns = field.shape
-    shape = (columns // J, steps * J, LANES)
+def to_blocks(first, second):
+    steps, _, _, columns = first.shape
+    shape = (columns // J, 2 * steps * J, LANES)
     return pl.pallas_call(
         scatter_kernel,
-        in_specs=[HBM],
+        in_specs=[HBM] * 2,
         out_specs=HBM,
         out_shape=pltpu.HBM(shape, F32),
         scratch_shapes=[
-            pltpu.VMEM((XB, steps, C, columns), F32),
+            pltpu.VMEM((2, XB, steps, C, columns), F32),
             pltpu.VMEM(shape, F32),
-            pltpu.SemaphoreType.DMA((XB,)),
+            pltpu.SemaphoreType.DMA((2, XB)),
             pltpu.SemaphoreType.DMA((SENT,)),
         ],
         compiler_params=PARAMS,
-    )(*in_hbm(field))
+    )(*in_hbm(first, second))
 
 
 def from_blocks(blocks):
@@ -301,148 +306,120 @@
     return z * cdf, slope
 
 
-def brick(ref, s):
-    return ref[:, s].reshape(-1, LANES)
-
-
-def forward_kernel(
-    x_ref, at, st, wt, fb,
-    coef1, coef2, slope1, slope2, x1h, x1l, x2h, x2l, mixed,
-):
-    bricks = x_ref.shape[1]
-    for s in range(bricks):
-        put_split(brick(x_ref, s), s, x1h, x1l)
-    analysis, synthesis = (at[0], at[1]), (st[0], st[1])
-
-    def first(s, z):
-        value, slope = gelu_parts(z)
-        slope1[s] = slope
-        put_split(value, s, x2h, x2l)
-
-    def second(s, z):
-        slope2[s] = gelu_parts(z)[1]
-
-    for l, (h, low, coef, emit) in enumerate(
-        ((x1h, x1l, coef1, first), (x2h, x2l, coef2, second))
-    ):
-        analyse(analysis, h, low, coef)
-        mix(coef, wt, l, mixed)
-        synthesise(synthesis, mixed, fb[l], h, low, emit)
-
-
-def forward(field, *tables):
-    _, bricks, _, _ = field.shape
-    _, modes, rows = tables[0].shape
-    coef = pltpu.HBM((bricks, modes, LANES), F32)
-    full = pltpu.HBM((bricks, rows, LANES), F32)
-    half = pltpu.HBM((bricks, rows, LANES), BF16)
-    return pl.pallas_call(
-        forward_kernel,
-        in_specs=[VMEM] * 5,
-        out_specs=[VMEM] * 8,
-        out_shape=[coef, coef, full, full, half, half, half, half],
-        scratch_shapes=[pltpu.VMEM((bricks, modes, LANES), F32)],
-        compiler_params=PARAMS,
-    )(field, *in_hbm(*tables))
-
-
-def backward_kernel(*refs):
-    g_any, slope1_any, slope2_any = refs[:3]
-    small_any = refs[3:7]
-    out_any, sens1_any, sens2_any = refs[7:10]
-    z_any = refs[10:14]
-    g, slope1, slope2 = refs[14:17]
-    small = refs[17:21]
-    sens1, sens2, z1h, z1l, z2h, z2l, out, mixed, load_sem, small_sem, store_sem = refs[21:]
-    at, st, wt, bb = small
-    bricks = slope1.shape[0]
+STORED = 4
+
+
+def layers_kernel(*refs):
+    both = refs[0]
+    small_any = refs[1:7]
+    out_any = refs[7]
+    kept_any = refs[8:20]
+    small = refs[20:26]
+    kept = refs[26:38]
+    field, sens, slope1, out, mixed, load_sem, small_sem, store_sem = refs[38:]
+    analysis_ref, synthesis_ref, mix_forward, mix_backward, band_forward, band_backward = small
+    coef1, coef2, sens1, sens2, x1h, x1l, x2h, x2l, z1h, z1l, z2h, z2l = kept
+    groups, bricks, lines, _ = both.shape
+    lines = lines // 2
     copy = pltpu.make_async_copy
 
+    tables = [copy(a, r, small_sem.at[i]) for i, (a, r) in enumerate(zip(small_any, small))]
     half = bricks // 2
-    loads = []
-    for i, part in enumerate((pl.ds(0, half), pl.ds(half, half))):
-        loads.append(copy(g_any.at[:, part], g.at[:, part], load_sem.at[2 * i]))
-        loads.append(copy(slope2_any.at[part], slope2.at[part], load_sem.at[2 * i + 1]))
-    loads.append(copy(slope1_any, slope1, load_sem.at[4]))
-    tables = [copy(a, r, small_sem.at[i]) for i, (a, r) in enumerate(zip(small_any, small))]
-    tables[0].start()
-    for load in loads[:4]:
+    loads = [
+        copy(both.at[:, at, pl.ds(0, lines)], field.at[:, at], load_sem.at[i])
+        for i, at in enumerate((pl.ds(0, half), pl.ds(half, half)))
+    ]
+    loads.append(copy(both.at[:, :, pl.ds(lines, lines)], sens, load_sem.at[2]))
+    for load in (tables[0], loads[0], loads[1], tables[2], tables[1], tables[4]):
         load.start()
-
     stores = []
 
     def store(source, target):
         stores.append(copy(source, target, store_sem.at[len(stores)]))
         stores[-1].start()
 
-    for load in (tables[0], loads[0], loads[1]):
-        load.wait()
-    for load in (tables[2], tables[1], tables[3], loads[4]):
-        load.start()
-    analysis = (at[0], at[1])
-    for s in range(0, bricks, 2):
-        if s == half:
-            for load in loads[2:4]:
-                load.wait()
-        for o in (s, s + 1):
-            put_split(brick(g, o) * slope2[o], o, z2h, z2l)
-        analyse_pair(analysis, z2h, z2l, sens2, s)
-    store(z2h, z_any[2])
-    store(z2l, z_any[3])
-    store(sens2, sens2_any)
-    tables[2].wait()
-    mix(sens2, wt, 1, mixed)
-    tables[1].wait()
-    tables[3].wait()
-    synthesis = (st[0], st[1])
-
-    def second(s, value):
-        if s == 0:
-            loads[4].wait()
+    def keep(*places):
+        for i in places:
+            store(kept[i], kept_any[i])
+
+    def brick(ref, s):
+        return ref[:, s].reshape(-1, LANES)
+
+    def first_out(s, value):
+        value, slope = gelu_parts(value)
+        slope1[s] = slope
+        put_split(value, s, x2h, x2l)
+
+    def second_out(s, value):
+        put_split(brick(sens, s) * gelu_parts(value)[1], s, z2h, z2l)
+
+    def second_back(s, value):
         put_split(value * slope1[s], s, z1h, z1l)
 
-    def first(s, value):
-        out[:, s] = value.reshape(out.shape[0], -1, LANES)
+    def first_back(s, value):
+        out[:, s] = value.reshape(groups, lines, LANES)
         if s % STORED == STORED - 1:
             done = pl.ds(s - STORED + 1, STORED)
             store(out.at[:, done], out_any.at[:, done])
 
-    synthesise(synthesis, mixed, bb[1], z2h, z2l, second)
-    store(z1h, z_any[0])
-    store(z1l, z_any[1])
+    tables[0].wait()
+    analysis = (analysis_ref[0], analysis_ref[1])
+    for s in range(0, bricks, 2):
+        if s % half == 0:
+            loads[s // half].wait()
+        for o in (s, s + 1):
+            put_split(brick(field, o), o, x1h, x1l)
+        analyse_pair(analysis, x1h, x1l, coef1, s)
+    for load in (loads[2], tables[3], tables[5]):
+        load.start()
+    keep(0, 4, 5)
+    tables[2].wait()
+    mix(coef1, mix_forward, 0, mixed)
+    tables[1].wait()
+    tables[4].wait()
+    synthesis = (synthesis_ref[0], synthesis_ref[1])
+    synthesise(synthesis, mixed, band_forward[0], x1h, x1l, first_out)
+    analyse(analysis, x2h, x2l, coef2)
+    keep(1, 6, 7)
+    mix(coef2, mix_forward, 1, mixed)
+    loads[2].wait()
+    synthesise(synthesis, mixed, band_forward[1], x2h, x2l, second_out)
+    analyse(analysis, z2h, z2l, sens2)
+    keep(3, 10, 11)
+    tables[3].wait()
+    mix(sens2, mix_backward, 1, mixed)
+    tables[5].wait()
+    synthesise(synthesis, mixed, band_backward[1], z2h, z2l, second_back)
     analyse(analysis, z1h, z1l, sens1)
-    store(sens1, sens1_any)
-    mix(sens1, wt, 0, mixed)
-    synthesise(synthesis, mixed, bb[0], z1h, z1l, first)
+    keep(2, 8, 9)
+    mix(sens1, mix_backward, 0, mixed)
+    synthesise(synthesis, mixed, band_backward[0], z1h, z1l, first_back)
     for done in stores:
         done.wait()
 
 
-STORED = 4
-
-
-def backward(cotangent, slope1, slope2, *tables):
-    groups, bricks, lines, _ = cotangent.shape
+def run_layers(both, *tables):
+    groups, bricks, lines, _ = both.shape
     _, modes, rows = tables[0].shape
     coef = ((bricks, modes, LANES), F32)
+    full = ((bricks, rows, LANES), F32)
     half = ((bricks, rows, LANES), BF16)
-    outs = [(cotangent.shape, F32), coef, coef, half, half, half, half]
-    operands = (cotangent, slope1, slope2, *tables)
-    scratch = [(o.shape, o.dtype) for o in operands]
-    scratch += [coef, coef, half, half, half, half, (cotangent.shape, F32), coef]
+    result = ((groups, bricks, lines // 2, LANES), F32)
+    kept = [coef] * 4 + [half] * 8
+    scratch = [(t.shape, t.dtype) for t in tables] + kept + [result, result, full, result, coef]
     return pl.pallas_call(
-        backward_kernel,
+        layers_kernel,
         in_specs=[ANY] + [HBM] * 6,
-        out_specs=[HBM] * 7,
-        out_shape=[pltpu.HBM(*o) for o in outs],
+        out_specs=[HBM] * 13,
+        out_shape=[pltpu.HBM(*o) for o in (result, *kept)],
         scratch_shapes=[pltpu.VMEM(*o) for o in scratch]
         + [
-            pltpu.SemaphoreType.DMA((5,)),
-            pltpu.SemaphoreType.DMA((4,)),
-            pltpu.SemaphoreType.DMA((6 + bricks // STORED,)),
+            pltpu.SemaphoreType.DMA((3,)),
+            pltpu.SemaphoreType.DMA((6,)),
+            pltpu.SemaphoreType.DMA((len(kept) + bricks // STORED,)),
         ],
         compiler_params=PARAMS,
-    )(cotangent, *in_hbm(*operands[1:]))
+    )(both, *in_hbm(*tables))
 
 
 ROWS = ((0,), (0,))
@@ -626,31 +603,16 @@
     scale = 2.0 / total_time
     exchange = functools.partial(lax.all_to_all, split_axis=0, concat_axis=0, tiled=True)
 
-    received = exchange(to_blocks(input_field), everyone)
-    cot_blocks = to_blocks(cotangent)
+    received = exchange(to_blocks(input_field, cotangent), everyone)
     prepared = prepare(scale, spectral_weights, conv_kernel, mode_list, total_time)
-    received, cot_blocks, prepared = lax.optimization_barrier((received, cot_blocks, prepared))
-    analysis, synthesis, mix_forward, mix_backward, band_forward, band_backward = prepared
-    cot_received = exchange(cot_blocks, everyone)
-    shape = (groups, bricks, steps * J, LANES)
-    coef1, coef2, slope1, slope2, x1h, x1l, x2h, x2l = forward(
-        received.reshape(shape), analysis, synthesis, mix_forward, band_forward
+    received, prepared = lax.optimization_barrier((received, prepared))
+    grad, *kept = run_layers(
+        received.reshape(groups, bricks, 2 * steps * J, LANES), *prepared
     )
-    grad, sens1, sens2, z1h, z1l, z2h, z2l = backward(
-        cot_received.reshape(shape),
-        slope1,
-        slope2,
-        analysis,
-        synthesis,
-        mix_backward,
-        band_backward,
-    )
-    returned = exchange(grad.reshape(cot_received.shape), everyone)
+    returned = exchange(grad.reshape(groups * bricks, steps * J, LANES), everyone)
     me = lax.axis_index("tm").astype(jnp.int32)
     place = jnp.stack([me // RADIX, me % RADIX])
-    pieces = weight_gradients(
-        scale, place, coef1, coef2, sens1, sens2, x1h, x1l, x2h, x2l, z1h, z1l, z2h, z2l
-    )
+    pieces = weight_gradients(scale, place, *kept)
     pieces = split_sum(shifted(pieces, "tm", groups, RADIX))
     grad_input, pieces = lax.optimization_barrier(
         (from_blocks(returned), shifted(pieces, "tm", groups, 1))

time: 147 us -> 144 us (0.980)
  waiting for transfers between devices: 52.2 us -> 61.8 us
  Pallas kernels: 53.4 us -> 46.3 us
  starting transfers between devices: 40.2 us -> 34.5 us
    all_to_all x3 -> x2, waiting for transfers between devices: 33.3 us -> 43 us  [the longest x1 43 us: on_device(): received = exchange(to_blocks(input_field, cotangent), everyone)]
    pallas_call x4 -> x2, Pallas kernels: 31.7 us -> 24.5 us  [the longest x1 19.9 us: run_layers(): pl.pallas_call(layers_kernel, in_specs=[ANY] + [HBM] * 6, out_specs=[HBM]...]
    all_to_all x3 -> x2, starting transfers between devices: 22.4 us -> 16.7 us  [the longest x1 11.7 us: on_device(): received = exchange(to_blocks(input_field, cotangent), everyone)]
  transfers between devices with their start and end apart: 13 -> 12, of which waited for: 6 -> 5; matrix products, arithmetic and copies ran while one was open for 0% -> 0% of each run, Pallas kernels for 25% -> 15%
where the time goes in v2:
time: 144 us
  waiting for transfers between devices  61.8 us (43%)
  Pallas kernels  46.3 us (32%)
  starting transfers between devices  34.5 us (24%)
    all_to_all x1, waiting for transfers between devices, on_device(): received = exchange(to_blocks(input_field, cotangent), everyone)  43 us
    pallas_call x1, Pallas kernels, run_layers(): pl.pallas_call(layers_kernel, in_specs=[ANY] + [HBM] * 6, out_specs=[HBM]...  19.9 us
    ppermute x10, waiting for transfers between devices, shifted(): got.append(lax.ppermute(pieces[r], axis, perm))  18.9 us
    ppermute x10, starting transfers between devices, shifted(): got.append(lax.ppermute(pieces[r], axis, perm))  17.8 us
    all_to_all x1, starting transfers between devices, on_device(): received = exchange(to_blocks(input_field, cotangent), everyone)  11.7 us
    pallas_call x1, Pallas kernels, weight_gradients(): pl.pallas_call(functools.partial(weight_kernel, scale), in_specs=[pl.Bloc...  9.69 us
    pallas_call x1, Pallas kernels, prepare(): pl.pallas_call(functools.partial(prepare_kernel, scale), in_specs=[VMEM]...  8.88 us
    all_to_all x1, starting transfers between devices, on_device(): exchange(grad.reshape(groups * bricks, steps * J, LANES), everyone)  5.05 us
  transfers between devices with their start and end apart: 12, of which 5 were waited for; matrix products, arithmetic and copies ran while one was open for 0% of the time, Pallas kernels for 15%

profile of v2, /device:TPU:0, one launch (start us, length us, event | category | flops | bytes accessed | tf_op | source)
XLA Modules:
  0.0 143.9 jit_solution(1895011484372858278)
XLA Ops:
  0.6 4.6 %shard_map.76 = f32[128,64,128]{2,1,0:T(8,128)} custom-call(f32[4,32,4,1024]{3,2,1,0:T(4,128)} %first_any.1, f32[4,32,4,1024]{3,2,1,0:T(4,128)} %second_any.1), custom_call_target="tpu_custom_call" | custom-call | tf_op jit(solution)/shard_map/pallas_call | solution.py:110
  5.3 0.0 copy-start.2
  5.3 0.0 copy-start
  5.3 0.0 copy-start.1
  5.3 11.7 %all-to-all-start = ((f32[128,64,128]{2,1,0:T(8,128)}), f32[128,64,128]{2,1,0:T(8,128)}, u32[]{:S(2)}, u32[]{:S(2)}) async-start(f32[128,64,128]{2,1,0:T(8,128)} %shard_map.76), calls=%async_computation | async-start | bytes 8388608 | tf_op jit(solution)/shard_map/all_to_all | solution.py:606
  17.0 0.0 copy-done.2
  17.0 0.1 fusion.6
  17.2 0.1 copy.11
  17.2 0.0 copy-done
  17.2 0.0 copy-done.1
  17.2 8.9 %shard_map.77 = (bf16[2,256,512]{2,1,0:T(8,128)(2,1)}, bf16[2,512,256]{2,1,0:T(8,128)(2,1)}, bf16[2,2,16,32,256]{4,3,2,1,0:T(8,128)(2,1)}, bf16[2,2,16,32,256]{4...) custom-call(f32[32,64]{1,0:T(8,128)S(1)} %bitcast.7, f32[64,32]{1,0:T(8,128)S(1)} %bitcast.8, ...), custom_call_target="tpu_custom_call" | custom-call | tf_op jit(solution)/shard_map/pallas_call | solution.py:209
  26.1 43.0 %all-to-all-done = f32[128,64,128]{2,1,0:T(8,128)} async-done(((f32[128,64,128]{2,1,0:T(8,128)}), f32[128,64,128]{2,1,0:T(8,128)}, u32[]{:S(2)}, u32[]{:S(2)}) %all-to-all-start) | async-done | bytes 4194336 | tf_op jit(solution)/shard_map/all_to_all | solution.py:606
  69.1 19.9 %shard_map.78 = (f32[16,8,32,128]{3,2,1,0:T(8,128)}, f32[8,256,128]{2,1,0:T(8,128)}, f32[8,256,128]{2,1,0:T(8,128)}, f32[8,256,128]{2,1,0:T(8,128)}, f32[8,256,1...) custom-call(f32[16,8,64,128]{3,2,1,0:T(8,128)} %bitcast.2.refs_0_, ...), custom_call_target="tpu_custom_call" | custom-call | tf_op jit(solution)/shard_map/pallas_call | solution.py:410
  89.0 5.0 %all-to-all-start.1 = ((f32[128,32,128]{2,1,0:T(8,128)}), f32[128,32,128]{2,1,0:T(8,128)S(1)}, u32[]{:S(2)}, u32[]{:S(2)}) async-start(f32[128,32,128]{2,1,0:T(8,128)} %bitcast.9), calls=%async_computation.1 | async-start | bytes 4194304 | tf_op jit(solution)/shard_map/all_to_all | solution.py:612
  94.1 0.1 pad_add_fusion.me_ref
  94.2 9.7 %shard_map.80 = (f32[176,128]{1,0:T(8,128)S(1)}, f32[176,128]{1,0:T(8,128)S(1)}, f32[176,128]{1,0:T(8,128)S(1)}, f32[176,128]{1,0:T(8,128)S(1)}) custom-call(s32[2]{0:T(128)S(1)} %pad_add_fusion.me_ref, f32[8,256,128]{2,1,0:T(8,128)} %get-tuple-element.58.refs_0_, f32[8,256,128]{2,1,0:T(8,128)} %get-tuple-element.59.refs_1_, ...), custom_call_target="tpu_custom_call" | custom-call | tf_op jit(solution)/shard_map/pallas_call | solution.py:515
  103.9 1.0 collective-permute-start
  104.9 2.7 %collective-permute-start.1 = (f32[176,128]{1,0:T(8,128)S(1)}, f32[176,128]{1,0:T(8,128)S(1)}, u32[]{:S(2)}, u32[]{:S(2)}) collective-permute-start(f32[176,128]{1,0:T(8,128)S(1)} %get-tuple-element.72), channel_id=1, source_target_pairs={{0,64},{8,72},{16,80},{24,88},{32,96},{40,104},{48,112},{56,120},{... | collective-permute-start | bytes 270344 | tf_op jit(solution)/shard_map/ppermute | solution.py:538
  107.6 1.5 %collective-permute-start.2 = (f32[176,128]{1,0:T(8,128)S(1)}, f32[176,128]{1,0:T(8,128)S(1)}, u32[]{:S(2)}, u32[]{:S(2)}) collective-permute-start(f32[176,128]{1,0:T(8,128)S(1)} %get-tuple-element.73), channel_id=1, source_target_pairs={{0,96},{8,104},{16,112},{24,120},{32,0},{40,8},{48,16},{56,24},{64... | collective-permute-start | bytes 270344 | tf_op jit(solution)/shard_map/ppermute | solution.py:538
  109.0 12.1 %collective-permute-done.refs_1_ = f32[176,128]{1,0:T(8,128)S(1)} collective-permute-done((f32[176,128]{1,0:T(8,128)S(1)}, f32[176,128]{1,0:T(8,128)S(1)}, u32[]{:S(2)}, u32[]{:S(2)}) %collective-permute-start) | collective-permute-done | bytes 90144 | tf_op jit(solution)/shard_map/ppermute | solution.py:538
  121.1 2.0 %collective-permute-done.1.refs_2_ = f32[176,128]{1,0:T(8,128)S(1)} collective-permute-done((f32[176,128]{1,0:T(8,128)S(1)}, f32[176,128]{1,0:T(8,128)S(1)}, u32[]{:S(2)}, u32[]{:S(2)}) %collective-permute-start.1) | collective-permute-done | bytes 90144 | tf_op jit(solution)/shard_map/ppermute | solution.py:538
  123.2 0.0 collective-permute-done.2.refs_3_
  123.2 0.1 collective-permute-start.3
  123.3 1.5 %collective-permute-start.4 = (f32[80,128]{1,0:T(8,128)S(1)}, f32[80,128]{1,0:T(8,128)S(1)}, u32[]{:S(2)}, u32[]{:S(2)}) collective-permute-start(f32[80,128]{1,0:T(8,128)S(1)} %get-tuple-element.76), channel_id=1, source_target_pairs={{0,16},{8,24},{16,0},{24,8},{32,48},{40,56},{48,32},{56,40},{64,80... | collective-permute-start | bytes 122888 | tf_op jit(solution)/shard_map/ppermute | solution.py:538
  124.9 1.4 collective-permute-start.5
  126.2 0.0 all-to-all-done.1.blocks_any
  126.2 2.4 %shard_map.79 = f32[4,32,4,1024]{3,2,1,0:T(4,128)} custom-call(f32[128,32,128]{2,1,0:T(8,128)S(1)} %all-to-all-done.1.blocks_any), custom_call_target="tpu_custom_call" | custom-call | tf_op jit(solution)/shard_map/pallas_call | solution.py:128
  128.6 0.0 collective-permute-done.3
  128.6 0.0 collective-permute-done.4
  128.6 0.0 collective-permute-done.5
  128.7 3.5 %collective-permute-start.6 = (f32[80,128]{1,0:T(8,128)S(1)}, f32[80,128]{1,0:T(8,128)S(1)}, u32[]{:S(2)}, u32[]{:S(2)}) collective-permute-start(f32[80,128]{1,0:T(8,128)S(1)} %add_add_fusion.1), channel_id=1, source_target_pairs={{0,4},{1,5},{2,6},{3,7},{4,0},{5,1},{6,2},{7,3},{8,12},{9,13},{10,... | collective-permute-start | bytes 122888 | tf_op jit(solution)/shard_map/ppermute | solution.py:538
  132.2 0.8 collective-permute-start.7
  133.0 2.4 %collective-permute-start.8 = (f32[80,128]{1,0:T(8,128)S(1)}, f32[80,128]{1,0:T(8,128)S(1)}, u32[]{:S(2)}, u32[]{:S(2)}) collective-permute-start(f32[80,128]{1,0:T(8,128)S(1)} %add_add_fusion.1), channel_id=1, source_target_pairs={{0,6},{1,7},{2,0},{3,1},{4,2},{5,3},{6,4},{7,5},{8,14},{9,15},{10,... | collective-permute-start | bytes 122888 | tf_op jit(solution)/shard_map/ppermute | solution.py:538
  135.4 0.0 collective-permute-done.6
  135.4 2.0 %collective-permute-done.7 = f32[80,128]{1,0:T(8,128)S(1)} collective-permute-done((f32[80,128]{1,0:T(8,128)S(1)}, f32[80,128]{1,0:T(8,128)S(1)}, u32[]{:S(2)}, u32[]{:S(2)}) %collective-permute-start.7) | collective-permute-done | bytes 40992 | tf_op jit(solution)/shard_map/ppermute | solution.py:538
  137.4 0.0 collective-permute-done.8
  137.4 2.9 %collective-permute-start.9 = (f32[80,128]{1,0:T(8,128)S(1)}, f32[80,128]{1,0:T(8,128)S(1)}, u32[]{:S(2)}, u32[]{:S(2)}) collective-permute-start(f32[80,128]{1,0:T(8,128)S(1)} %add_add_fusion.one_ref), channel_id=1, source_target_pairs={{0,1},{1,0},{2,3},{3,2},{4,5},{5,4},{6,7},{7,6},{8,9},{9,8},{10,11... | collective-permute-start | bytes 122888 | tf_op jit(solution)/shard_map/ppermute | solution.py:538
  140.3 2.7 %collective-permute-done.9.other_ref = f32[80,128]{1,0:T(8,128)S(1)} collective-permute-done((f32[80,128]{1,0:T(8,128)S(1)}, f32[80,128]{1,0:T(8,128)S(1)}, u32[]{:S(2)}, u32[]{:S(2)}) %collective-permute-start.9) | collective-permute-done | bytes 40992 | tf_op jit(solution)/shard_map/ppermute | solution.py:538
  143.0 0.9 shard_map.82
  (5 shorter events, 0.1 us)
Async XLA Ops:
  5.3 11.7 %copy-start.2 = (s32[16]{0:T(128)S(1)}, s32[16]{0:T(128)}, u32[]{:S(2)}) copy-start(s32[16]{0:T(128)} %param.9) | copy-start | bytes 196
  5.3 12.0 %copy-start = (f32[2,2,16,32,32]{4,3,2,1,0:T(8,128)S(1)}, f32[2,2,16,32,32]{4,3,2,1,0:T(8,128)}, u32[]{:S(2)}) copy-start(f32[2,2,16,32,32]{4,3,2,1,0:T(8,128)} %w_ref.1) | copy-start | bytes 786436
  5.3 12.0 %copy-start.1 = (f32[2,3,32,32]{3,2,1,0:T(8,128)S(1)}, f32[2,3,32,32]{3,2,1,0:T(8,128)}, u32[]{:S(2)}) copy-start(f32[2,3,32,32]{3,2,1,0:T(8,128)} %k_ref.1) | copy-start | bytes 73732
  5.3 63.8 %all-to-all-start = ((f32[128,64,128]{2,1,0:T(8,128)}), f32[128,64,128]{2,1,0:T(8,128)}, u32[]{:S(2)}, u32[]{:S(2)}) async-start(f32[128,64,128]{2,1,0:T(8,128)} %shard_map.76), calls=%async_computation | async-start | bytes 8388608 | tf_op jit(solution)/shard_map/all_to_all | solution.py:606
  89.0 37.2 %all-to-all-start.1 = ((f32[128,32,128]{2,1,0:T(8,128)}), f32[128,32,128]{2,1,0:T(8,128)S(1)}, u32[]{:S(2)}, u32[]{:S(2)}) async-start(f32[128,32,128]{2,1,0:T(8,128)} %bitcast.9), calls=%async_computation.1 | async-start | bytes 4194304 | tf_op jit(solution)/shard_map/all_to_all | solution.py:612
  103.9 17.3 %collective-permute-start = (f32[176,128]{1,0:T(8,128)S(1)}, f32[176,128]{1,0:T(8,128)S(1)}, u32[]{:S(2)}, u32[]{:S(2)}) collective-permute-start(f32[176,128]{1,0:T(8,128)S(1)} %get-tuple-element.71), channel_id=1, source_target_pairs={{0,32},{8,40},{16,48},{24,56},{32,64},{40,72},{48,80},{56,88},{64,... | collective-permute-start | bytes 270344 | tf_op jit(solution)/shard_map/ppermute | solution.py:538
  104.9 18.3 %collective-permute-start.1 = (f32[176,128]{1,0:T(8,128)S(1)}, f32[176,128]{1,0:T(8,128)S(1)}, u32[]{:S(2)}, u32[]{:S(2)}) collective-permute-start(f32[176,128]{1,0:T(8,128)S(1)} %get-tuple-element.72), channel_id=1, source_target_pairs={{0,64},{8,72},{16,80},{24,88},{32,96},{40,104},{48,112},{56,120},{... | collective-permute-start | bytes 270344 | tf_op jit(solution)/shard_map/ppermute | solution.py:538
  107.6 15.6 %collective-permute-start.2 = (f32[176,128]{1,0:T(8,128)S(1)}, f32[176,128]{1,0:T(8,128)S(1)}, u32[]{:S(2)}, u32[]{:S(2)}) collective-permute-start(f32[176,128]{1,0:T(8,128)S(1)} %get-tuple-element.73), channel_id=1, source_target_pairs={{0,96},{8,104},{16,112},{24,120},{32,0},{40,8},{48,16},{56,24},{64... | collective-permute-start | bytes 270344 | tf_op jit(solution)/shard_map/ppermute | solution.py:538
  123.2 5.4 %collective-permute-start.3 = (f32[80,128]{1,0:T(8,128)S(1)}, f32[80,128]{1,0:T(8,128)S(1)}, u32[]{:S(2)}, u32[]{:S(2)}) collective-permute-start(f32[80,128]{1,0:T(8,128)S(1)} %get-tuple-element.75), channel_id=1, source_target_pairs={{0,8},{8,16},{16,24},{24,0},{32,40},{40,48},{48,56},{56,32},{64,72... | collective-permute-start | bytes 122888 | tf_op jit(solution)/shard_map/ppermute | solution.py:538
  123.3 5.3 %collective-permute-start.4 = (f32[80,128]{1,0:T(8,128)S(1)}, f32[80,128]{1,0:T(8,128)S(1)}, u32[]{:S(2)}, u32[]{:S(2)}) collective-permute-start(f32[80,128]{1,0:T(8,128)S(1)} %get-tuple-element.76), channel_id=1, source_target_pairs={{0,16},{8,24},{16,0},{24,8},{32,48},{40,56},{48,32},{56,40},{64,80... | collective-permute-start | bytes 122888 | tf_op jit(solution)/shard_map/ppermute | solution.py:538
  124.9 3.8 %collective-permute-start.5 = (f32[80,128]{1,0:T(8,128)S(1)}, f32[80,128]{1,0:T(8,128)S(1)}, u32[]{:S(2)}, u32[]{:S(2)}) collective-permute-start(f32[80,128]{1,0:T(8,128)S(1)} %get-tuple-element.77), channel_id=1, source_target_pairs={{0,24},{8,0},{16,8},{24,16},{32,56},{40,32},{48,40},{56,48},{64,88... | collective-permute-start | bytes 122888 | tf_op jit(solution)/shard_map/ppermute | solution.py:538
  128.7 6.8 %collective-permute-start.6 = (f32[80,128]{1,0:T(8,128)S(1)}, f32[80,128]{1,0:T(8,128)S(1)}, u32[]{:S(2)}, u32[]{:S(2)}) collective-permute-start(f32[80,128]{1,0:T(8,128)S(1)} %add_add_fusion.1), channel_id=1, source_target_pairs={{0,4},{1,5},{2,6},{3,7},{4,0},{5,1},{6,2},{7,3},{8,12},{9,13},{10,... | collective-permute-start | bytes 122888 | tf_op jit(solution)/shard_map/ppermute | solution.py:538
  132.2 5.2 %collective-permute-start.7 = (f32[80,128]{1,0:T(8,128)S(1)}, f32[80,128]{1,0:T(8,128)S(1)}, u32[]{:S(2)}, u32[]{:S(2)}) collective-permute-start(f32[80,128]{1,0:T(8,128)S(1)} %add_add_fusion.1), channel_id=1, source_target_pairs={{0,2},{1,3},{2,4},{3,5},{4,6},{5,7},{6,0},{7,1},{8,10},{9,11},{10,... | collective-permute-start | bytes 122888 | tf_op jit(solution)/shard_map/ppermute | solution.py:538
  133.0 4.4 %collective-permute-start.8 = (f32[80,128]{1,0:T(8,128)S(1)}, f32[80,128]{1,0:T(8,128)S(1)}, u32[]{:S(2)}, u32[]{:S(2)}) collective-permute-start(f32[80,128]{1,0:T(8,128)S(1)} %add_add_fusion.1), channel_id=1, source_target_pairs={{0,6},{1,7},{2,0},{3,1},{4,2},{5,3},{6,4},{7,5},{8,14},{9,15},{10,... | collective-permute-start | bytes 122888 | tf_op jit(solution)/shard_map/ppermute | solution.py:538
  137.4 5.6 %collective-permute-start.9 = (f32[80,128]{1,0:T(8,128)S(1)}, f32[80,128]{1,0:T(8,128)S(1)}, u32[]{:S(2)}, u32[]{:S(2)}) collective-permute-start(f32[80,128]{1,0:T(8,128)S(1)} %add_add_fusion.one_ref), channel_id=1, source_target_pairs={{0,1},{1,0},{2,3},{3,2},{4,5},{5,4},{6,7},{7,6},{8,9},{9,8},{10,11... | collective-permute-start | bytes 122888 | tf_op jit(solution)/shard_map/ppermute | solution.py:538

commit v3 on v2

--- a/solution.py
+++ b/solution.py
@@ -266,28 +266,29 @@
         analyse_pair(table, high_ref, low_ref, coef_ref, s)
 
 
-def mixing_matrix(w_ref, piece, l, m):
+def mixing_rows(w_ref, piece, l, m):
     row = lax.broadcasted_iota(jnp.int32, (LANES, 2 * LANES), 0) // C
     col = lax.broadcasted_iota(jnp.int32, (LANES, 2 * LANES), 1) // C % XB
     wide = jnp.concatenate([w_ref[piece, l, m]] * XB, axis=0)
-    top = jnp.where(row == col, wide, jnp.zeros_like(wide))
-    return jnp.concatenate(
-        [top, jnp.concatenate([-top[:, LANES:], top[:, :LANES]], axis=1)], axis=0
-    )
+    return jnp.where(row == col, wide, jnp.zeros_like(wide))
 
 
 def mix(coef_ref, w_ref, l, mixed_ref):
     bricks = coef_ref.shape[0]
+    rows = bricks * J
     for m in range(w_ref.shape[2]):
         re, im = slice(2 * J * m, 2 * J * m + J), slice(2 * J * m + J, 2 * J * (m + 1))
-        value = jnp.concatenate(
-            [coef_ref[:, re].reshape(bricks * J, LANES), coef_ref[:, im].reshape(bricks * J, LANES)],
-            axis=1,
+        rh, rl = split(coef_ref[:, re].reshape(rows, LANES))
+        ih, il = split(coef_ref[:, im].reshape(rows, LANES))
+        left = jnp.concatenate([rh, ih, rl, il], axis=0)
+        matrix = jnp.concatenate([mixing_rows(w_ref, piece, l, m) for piece in range(2)], axis=0)
+        product = jnp.dot(
+            jnp.concatenate([left, left], axis=1), matrix, preferred_element_type=F32
         )
-        matrix = tuple(mixing_matrix(w_ref, piece, l, m) for piece in range(2))
-        result = dot3(split(value), matrix)
-        mixed_ref[:, re] = result[:, :LANES].reshape(bricks, J, LANES)
-        mixed_ref[:, im] = result[:, LANES:].reshape(bricks, J, LANES)
+        a = product[:rows] + product[2 * rows : 3 * rows]
+        b = product[rows : 2 * rows] + product[3 * rows :]
+        mixed_ref[:, re] = (a[:, :LANES] - b[:, LANES:]).reshape(bricks, J, LANES)
+        mixed_ref[:, im] = (a[:, LANES:] + b[:, :LANES]).reshape(bricks, J, LANES)
 
 
 def synthesise(table, mixed_ref, matrix, high_ref, low_ref, emit):

time: 144 us -> 142 us (0.986)
  Pallas kernels: 46.3 us -> 44.2 us
    pallas_call x1, Pallas kernels: 19.9 us -> 17.8 us  [run_layers(): pl.pallas_call(layers_kernel, in_specs=[ANY] + [HBM] * 6, out_specs=[HBM]...]
where the time goes in v3:
time: 142 us
  waiting for transfers between devices  61.8 us (44%)
  Pallas kernels  44.2 us (31%)
  starting transfers between devices  34.5 us (24%)
    all_to_all x1, waiting for transfers between devices, on_device(): received = exchange(to_blocks(input_field, cotangent), everyone)  43 us
    ppermute x10, waiting for transfers between devices, shifted(): got.append(lax.ppermute(pieces[r], axis, perm))  18.9 us
    ppermute x10, starting transfers between devices, shifted(): got.append(lax.ppermute(pieces[r], axis, perm))  17.8 us
    pallas_call x1, Pallas kernels, run_layers(): pl.pallas_call(layers_kernel, in_specs=[ANY] + [HBM] * 6, out_specs=[HBM]...  17.8 us
    all_to_all x1, starting transfers between devices, on_device(): received = exchange(to_blocks(input_field, cotangent), everyone)  11.7 us
    pallas_call x1, Pallas kernels, weight_gradients(): pl.pallas_call(functools.partial(weight_kernel, scale), in_specs=[pl.Bloc...  9.69 us
    pallas_call x1, Pallas kernels, prepare(): pl.pallas_call(functools.partial(prepare_kernel, scale), in_specs=[VMEM]...  8.88 us
    all_to_all x1, starting transfers between devices, on_device(): exchange(grad.reshape(groups * bricks, steps * J, LANES), everyone)  5.01 us
  transfers between devices with their start and end apart: 12, of which 5 were waited for; matrix products, arithmetic and copies ran while one was open for 0% of the time, Pallas kernels for 15%

profile of v3, /device:TPU:0, one launch (start us, length us, event | category | flops | bytes accessed | tf_op | source)
XLA Modules:
  0.0 141.7 jit_solution(128555944262538060)
XLA Ops:
  0.6 4.6 %shard_map.76 = f32[128,64,128]{2,1,0:T(8,128)} custom-call(f32[4,32,4,1024]{3,2,1,0:T(4,128)} %first_any.1, f32[4,32,4,1024]{3,2,1,0:T(4,128)} %second_any.1), custom_call_target="tpu_custom_call" | custom-call | tf_op jit(solution)/shard_map/pallas_call | solution.py:110
  5.3 0.0 copy-start.2
  5.3 0.0 copy-start
  5.3 0.0 copy-start.1
  5.3 11.7 %all-to-all-start = ((f32[128,64,128]{2,1,0:T(8,128)}), f32[128,64,128]{2,1,0:T(8,128)}, u32[]{:S(2)}, u32[]{:S(2)}) async-start(f32[128,64,128]{2,1,0:T(8,128)} %shard_map.76), calls=%async_computation | async-start | bytes 8388608 | tf_op jit(solution)/shard_map/all_to_all | solution.py:607
  17.0 0.0 copy-done.2
  17.0 0.1 fusion.6
  17.2 0.1 copy.11
  17.2 0.0 copy-done
  17.2 0.0 copy-done.1
  17.2 8.9 %shard_map.77 = (bf16[2,256,512]{2,1,0:T(8,128)(2,1)}, bf16[2,512,256]{2,1,0:T(8,128)(2,1)}, bf16[2,2,16,32,256]{4,3,2,1,0:T(8,128)(2,1)}, bf16[2,2,16,32,256]{4...) custom-call(f32[32,64]{1,0:T(8,128)S(1)} %bitcast.7, f32[64,32]{1,0:T(8,128)S(1)} %bitcast.8, ...), custom_call_target="tpu_custom_call" | custom-call | tf_op jit(solution)/shard_map/pallas_call | solution.py:209
  26.1 43.0 %all-to-all-done = f32[128,64,128]{2,1,0:T(8,128)} async-done(((f32[128,64,128]{2,1,0:T(8,128)}), f32[128,64,128]{2,1,0:T(8,128)}, u32[]{:S(2)}, u32[]{:S(2)}) %all-to-all-start) | async-done | bytes 4194336 | tf_op jit(solution)/shard_map/all_to_all | solution.py:607
  69.1 17.8 %shard_map.78 = (f32[16,8,32,128]{3,2,1,0:T(8,128)}, f32[8,256,128]{2,1,0:T(8,128)}, f32[8,256,128]{2,1,0:T(8,128)}, f32[8,256,128]{2,1,0:T(8,128)}, f32[8,256,1...) custom-call(f32[16,8,64,128]{3,2,1,0:T(8,128)} %bitcast.2.refs_0_, ...), custom_call_target="tpu_custom_call" | custom-call | tf_op jit(solution)/shard_map/pallas_call | solution.py:411
  86.9 5.0 %all-to-all-start.1 = ((f32[128,32,128]{2,1,0:T(8,128)}), f32[128,32,128]{2,1,0:T(8,128)S(1)}, u32[]{:S(2)}, u32[]{:S(2)}) async-start(f32[128,32,128]{2,1,0:T(8,128)} %bitcast.9), calls=%async_computation.1 | async-start | bytes 4194304 | tf_op jit(solution)/shard_map/all_to_all | solution.py:613
  91.9 0.1 pad_add_fusion.me_ref
  92.0 9.7 %shard_map.80 = (f32[176,128]{1,0:T(8,128)S(1)}, f32[176,128]{1,0:T(8,128)S(1)}, f32[176,128]{1,0:T(8,128)S(1)}, f32[176,128]{1,0:T(8,128)S(1)}) custom-call(s32[2]{0:T(128)S(1)} %pad_add_fusion.me_ref, f32[8,256,128]{2,1,0:T(8,128)} %get-tuple-element.58.refs_0_, f32[8,256,128]{2,1,0:T(8,128)} %get-tuple-element.59.refs_1_, ...), custom_call_target="tpu_custom_call" | custom-call | tf_op jit(solution)/shard_map/pallas_call | solution.py:516
  101.7 1.0 collective-permute-start
  102.7 2.7 %collective-permute-start.1 = (f32[176,128]{1,0:T(8,128)S(1)}, f32[176,128]{1,0:T(8,128)S(1)}, u32[]{:S(2)}, u32[]{:S(2)}) collective-permute-start(f32[176,128]{1,0:T(8,128)S(1)} %get-tuple-element.72), channel_id=1, source_target_pairs={{0,64},{8,72},{16,80},{24,88},{32,96},{40,104},{48,112},{56,120},{... | collective-permute-start | bytes 270344 | tf_op jit(solution)/shard_map/ppermute | solution.py:539
  105.4 1.5 %collective-permute-start.2 = (f32[176,128]{1,0:T(8,128)S(1)}, f32[176,128]{1,0:T(8,128)S(1)}, u32[]{:S(2)}, u32[]{:S(2)}) collective-permute-start(f32[176,128]{1,0:T(8,128)S(1)} %get-tuple-element.73), channel_id=1, source_target_pairs={{0,96},{8,104},{16,112},{24,120},{32,0},{40,8},{48,16},{56,24},{64... | collective-permute-start | bytes 270344 | tf_op jit(solution)/shard_map/ppermute | solution.py:539
  106.8 12.1 %collective-permute-done.refs_1_ = f32[176,128]{1,0:T(8,128)S(1)} collective-permute-done((f32[176,128]{1,0:T(8,128)S(1)}, f32[176,128]{1,0:T(8,128)S(1)}, u32[]{:S(2)}, u32[]{:S(2)}) %collective-permute-start) | collective-permute-done | bytes 90144 | tf_op jit(solution)/shard_map/ppermute | solution.py:539
  119.0 2.0 %collective-permute-done.1.refs_2_ = f32[176,128]{1,0:T(8,128)S(1)} collective-permute-done((f32[176,128]{1,0:T(8,128)S(1)}, f32[176,128]{1,0:T(8,128)S(1)}, u32[]{:S(2)}, u32[]{:S(2)}) %collective-permute-start.1) | collective-permute-done | bytes 90144 | tf_op jit(solution)/shard_map/ppermute | solution.py:539
  121.0 0.0 collective-permute-done.2.refs_3_
  121.0 0.1 collective-permute-start.3
  121.1 1.5 %collective-permute-start.4 = (f32[80,128]{1,0:T(8,128)S(1)}, f32[80,128]{1,0:T(8,128)S(1)}, u32[]{:S(2)}, u32[]{:S(2)}) collective-permute-start(f32[80,128]{1,0:T(8,128)S(1)} %get-tuple-element.76), channel_id=1, source_target_pairs={{0,16},{8,24},{16,0},{24,8},{32,48},{40,56},{48,32},{56,40},{64,80... | collective-permute-start | bytes 122888 | tf_op jit(solution)/shard_map/ppermute | solution.py:539
  122.7 1.4 collective-permute-start.5
  124.0 0.0 all-to-all-done.1.blocks_any
  124.0 2.4 %shard_map.79 = f32[4,32,4,1024]{3,2,1,0:T(4,128)} custom-call(f32[128,32,128]{2,1,0:T(8,128)S(1)} %all-to-all-done.1.blocks_any), custom_call_target="tpu_custom_call" | custom-call | tf_op jit(solution)/shard_map/pallas_call | solution.py:128
  126.4 0.0 collective-permute-done.3
  126.4 0.0 collective-permute-done.4
  126.4 0.0 collective-permute-done.5
  126.5 3.5 %collective-permute-start.6 = (f32[80,128]{1,0:T(8,128)S(1)}, f32[80,128]{1,0:T(8,128)S(1)}, u32[]{:S(2)}, u32[]{:S(2)}) collective-permute-start(f32[80,128]{1,0:T(8,128)S(1)} %add_add_fusion.1), channel_id=1, source_target_pairs={{0,4},{1,5},{2,6},{3,7},{4,0},{5,1},{6,2},{7,3},{8,12},{9,13},{10,... | collective-permute-start | bytes 122888 | tf_op jit(solution)/shard_map/ppermute | solution.py:539
  130.0 0.8 collective-permute-start.7
  130.8 2.4 %collective-permute-start.8 = (f32[80,128]{1,0:T(8,128)S(1)}, f32[80,128]{1,0:T(8,128)S(1)}, u32[]{:S(2)}, u32[]{:S(2)}) collective-permute-start(f32[80,128]{1,0:T(8,128)S(1)} %add_add_fusion.1), channel_id=1, source_target_pairs={{0,6},{1,7},{2,0},{3,1},{4,2},{5,3},{6,4},{7,5},{8,14},{9,15},{10,... | collective-permute-start | bytes 122888 | tf_op jit(solution)/shard_map/ppermute | solution.py:539
  133.2 0.0 collective-permute-done.6
  133.2 2.0 %collective-permute-done.7 = f32[80,128]{1,0:T(8,128)S(1)} collective-permute-done((f32[80,128]{1,0:T(8,128)S(1)}, f32[80,128]{1,0:T(8,128)S(1)}, u32[]{:S(2)}, u32[]{:S(2)}) %collective-permute-start.7) | collective-permute-done | bytes 40992 | tf_op jit(solution)/shard_map/ppermute | solution.py:539
  135.2 0.0 collective-permute-done.8
  135.2 2.9 %collective-permute-start.9 = (f32[80,128]{1,0:T(8,128)S(1)}, f32[80,128]{1,0:T(8,128)S(1)}, u32[]{:S(2)}, u32[]{:S(2)}) collective-permute-start(f32[80,128]{1,0:T(8,128)S(1)} %add_add_fusion.one_ref), channel_id=1, source_target_pairs={{0,1},{1,0},{2,3},{3,2},{4,5},{5,4},{6,7},{7,6},{8,9},{9,8},{10,11... | collective-permute-start | bytes 122888 | tf_op jit(solution)/shard_map/ppermute | solution.py:539
  138.1 2.7 %collective-permute-done.9.other_ref = f32[80,128]{1,0:T(8,128)S(1)} collective-permute-done((f32[80,128]{1,0:T(8,128)S(1)}, f32[80,128]{1,0:T(8,128)S(1)}, u32[]{:S(2)}, u32[]{:S(2)}) %collective-permute-start.9) | collective-permute-done | bytes 40992 | tf_op jit(solution)/shard_map/ppermute | solution.py:539
  140.8 0.9 shard_map.82
  (5 shorter events, 0.1 us)
Async XLA Ops:
  5.3 11.7 %copy-start.2 = (s32[16]{0:T(128)S(1)}, s32[16]{0:T(128)}, u32[]{:S(2)}) copy-start(s32[16]{0:T(128)} %param.9) | copy-start | bytes 196
  5.3 12.0 %copy-start = (f32[2,2,16,32,32]{4,3,2,1,0:T(8,128)S(1)}, f32[2,2,16,32,32]{4,3,2,1,0:T(8,128)}, u32[]{:S(2)}) copy-start(f32[2,2,16,32,32]{4,3,2,1,0:T(8,128)} %w_ref.1) | copy-start | bytes 786436
  5.3 12.0 %copy-start.1 = (f32[2,3,32,32]{3,2,1,0:T(8,128)S(1)}, f32[2,3,32,32]{3,2,1,0:T(8,128)}, u32[]{:S(2)}) copy-start(f32[2,3,32,32]{3,2,1,0:T(8,128)} %k_ref.1) | copy-start | bytes 73732
  5.3 63.8 %all-to-all-start = ((f32[128,64,128]{2,1,0:T(8,128)}), f32[128,64,128]{2,1,0:T(8,128)}, u32[]{:S(2)}, u32[]{:S(2)}) async-start(f32[128,64,128]{2,1,0:T(8,128)} %shard_map.76), calls=%async_computation | async-start | bytes 8388608 | tf_op jit(solution)/shard_map/all_to_all | solution.py:607
  86.9 37.2 %all-to-all-start.1 = ((f32[128,32,128]{2,1,0:T(8,128)}), f32[128,32,128]{2,1,0:T(8,128)S(1)}, u32[]{:S(2)}, u32[]{:S(2)}) async-start(f32[128,32,128]{2,1,0:T(8,128)} %bitcast.9), calls=%async_computation.1 | async-start | bytes 4194304 | tf_op jit(solution)/shard_map/all_to_all | solution.py:613
  101.7 17.3 %collective-permute-start = (f32[176,128]{1,0:T(8,128)S(1)}, f32[176,128]{1,0:T(8,128)S(1)}, u32[]{:S(2)}, u32[]{:S(2)}) collective-permute-start(f32[176,128]{1,0:T(8,128)S(1)} %get-tuple-element.71), channel_id=1, source_target_pairs={{0,32},{8,40},{16,48},{24,56},{32,64},{40,72},{48,80},{56,88},{64,... | collective-permute-start | bytes 270344 | tf_op jit(solution)/shard_map/ppermute | solution.py:539
  102.7 18.3 %collective-permute-start.1 = (f32[176,128]{1,0:T(8,128)S(1)}, f32[176,128]{1,0:T(8,128)S(1)}, u32[]{:S(2)}, u32[]{:S(2)}) collective-permute-start(f32[176,128]{1,0:T(8,128)S(1)} %get-tuple-element.72), channel_id=1, source_target_pairs={{0,64},{8,72},{16,80},{24,88},{32,96},{40,104},{48,112},{56,120},{... | collective-permute-start | bytes 270344 | tf_op jit(solution)/shard_map/ppermute | solution.py:539
  105.4 15.6 %collective-permute-start.2 = (f32[176,128]{1,0:T(8,128)S(1)}, f32[176,128]{1,0:T(8,128)S(1)}, u32[]{:S(2)}, u32[]{:S(2)}) collective-permute-start(f32[176,128]{1,0:T(8,128)S(1)} %get-tuple-element.73), channel_id=1, source_target_pairs={{0,96},{8,104},{16,112},{24,120},{32,0},{40,8},{48,16},{56,24},{64... | collective-permute-start | bytes 270344 | tf_op jit(solution)/shard_map/ppermute | solution.py:539
  121.0 5.4 %collective-permute-start.3 = (f32[80,128]{1,0:T(8,128)S(1)}, f32[80,128]{1,0:T(8,128)S(1)}, u32[]{:S(2)}, u32[]{:S(2)}) collective-permute-start(f32[80,128]{1,0:T(8,128)S(1)} %get-tuple-element.75), channel_id=1, source_target_pairs={{0,8},{8,16},{16,24},{24,0},{32,40},{40,48},{48,56},{56,32},{64,72... | collective-permute-start | bytes 122888 | tf_op jit(solution)/shard_map/ppermute | solution.py:539
  121.1 5.3 %collective-permute-start.4 = (f32[80,128]{1,0:T(8,128)S(1)}, f32[80,128]{1,0:T(8,128)S(1)}, u32[]{:S(2)}, u32[]{:S(2)}) collective-permute-start(f32[80,128]{1,0:T(8,128)S(1)} %get-tuple-element.76), channel_id=1, source_target_pairs={{0,16},{8,24},{16,0},{24,8},{32,48},{40,56},{48,32},{56,40},{64,80... | collective-permute-start | bytes 122888 | tf_op jit(solution)/shard_map/ppermute | solution.py:539
  122.7 3.8 %collective-permute-start.5 = (f32[80,128]{1,0:T(8,128)S(1)}, f32[80,128]{1,0:T(8,128)S(1)}, u32[]{:S(2)}, u32[]{:S(2)}) collective-permute-start(f32[80,128]{1,0:T(8,128)S(1)} %get-tuple-element.77), channel_id=1, source_target_pairs={{0,24},{8,0},{16,8},{24,16},{32,56},{40,32},{48,40},{56,48},{64,88... | collective-permute-start | bytes 122888 | tf_op jit(solution)/shard_map/ppermute | solution.py:539
  126.5 6.8 %collective-permute-start.6 = (f32[80,128]{1,0:T(8,128)S(1)}, f32[80,128]{1,0:T(8,128)S(1)}, u32[]{:S(2)}, u32[]{:S(2)}) collective-permute-start(f32[80,128]{1,0:T(8,128)S(1)} %add_add_fusion.1), channel_id=1, source_target_pairs={{0,4},{1,5},{2,6},{3,7},{4,0},{5,1},{6,2},{7,3},{8,12},{9,13},{10,... | collective-permute-start | bytes 122888 | tf_op jit(solution)/shard_map/ppermute | solution.py:539
  130.0 5.2 %collective-permute-start.7 = (f32[80,128]{1,0:T(8,128)S(1)}, f32[80,128]{1,0:T(8,128)S(1)}, u32[]{:S(2)}, u32[]{:S(2)}) collective-permute-start(f32[80,128]{1,0:T(8,128)S(1)} %add_add_fusion.1), channel_id=1, source_target_pairs={{0,2},{1,3},{2,4},{3,5},{4,6},{5,7},{6,0},{7,1},{8,10},{9,11},{10,... | collective-permute-start | bytes 122888 | tf_op jit(solution)/shard_map/ppermute | solution.py:539
  130.8 4.4 %collective-permute-start.8 = (f32[80,128]{1,0:T(8,128)S(1)}, f32[80,128]{1,0:T(8,128)S(1)}, u32[]{:S(2)}, u32[]{:S(2)}) collective-permute-start(f32[80,128]{1,0:T(8,128)S(1)} %add_add_fusion.1), channel_id=1, source_target_pairs={{0,6},{1,7},{2,0},{3,1},{4,2},{5,3},{6,4},{7,5},{8,14},{9,15},{10,... | collective-permute-start | bytes 122888 | tf_op jit(solution)/shard_map/ppermute | solution.py:539
  135.2 5.6 %collective-permute-start.9 = (f32[80,128]{1,0:T(8,128)S(1)}, f32[80,128]{1,0:T(8,128)S(1)}, u32[]{:S(2)}, u32[]{:S(2)}) collective-permute-start(f32[80,128]{1,0:T(8,128)S(1)} %add_add_fusion.one_ref), channel_id=1, source_target_pairs={{0,1},{1,0},{2,3},{3,2},{4,5},{5,4},{6,7},{7,6},{8,9},{9,8},{10,11... | collective-permute-start | bytes 122888 | tf_op jit(solution)/shard_map/ppermute | solution.py:539

commit v4 on v3

--- a/solution.py
+++ b/solution.py
@@ -66,11 +66,15 @@
                 rows = jnp.concatenate([field[which, x, t, :, lanes] for x in range(XB)], axis=0)
                 rows = rows.T.reshape(groups, J, LANES)
                 out[q * groups : (q + 1) * groups, at : at + J] = rows
-            if which == 1 and (q + 1) % (count // SENT) == 0:
+            if (q + 1) % (count // SENT) == 0:
                 size = groups * count // SENT
                 part = pl.ds((q + 1) * groups - size, size)
-                sem = store_sem.at[len(stores)]
-                stores.append(pltpu.make_async_copy(out.at[part], out_any.at[part], sem))
+                lines = pl.ds(which * steps * J, steps * J)
+                stores.append(
+                    pltpu.make_async_copy(
+                        out.at[part, lines], out_any.at[part, lines], store_sem.at[len(stores)]
+                    )
+                )
                 stores[-1].start()
     for store in stores:
         store.wait()
@@ -116,7 +120,7 @@
             pltpu.VMEM((2, XB, steps, C, columns), F32),
             pltpu.VMEM(shape, F32),
             pltpu.SemaphoreType.DMA((2, XB)),
-            pltpu.SemaphoreType.DMA((SENT,)),
+            pltpu.SemaphoreType.DMA((2 * SENT,)),
         ],
         compiler_params=PARAMS,
     )(*in_hbm(first, second))

time: 142 us -> 141 us (level)
  no operation moved by 1% of the time
where the time goes in v4:
time: 141 us
  waiting for transfers between devices  61.8 us (44%)
  Pallas kernels  43.6 us (31%)
  starting transfers between devices  34.5 us (24%)
    all_to_all x1, waiting for transfers between devices, on_device(): received = exchange(to_blocks(input_field, cotangent), everyone)  43 us
    ppermute x10, waiting for transfers between devices, shifted(): got.append(lax.ppermute(pieces[r], axis, perm))  18.9 us
    ppermute x10, starting transfers between devices, shifted(): got.append(lax.ppermute(pieces[r], axis, perm))  17.8 us
    pallas_call x1, Pallas kernels, run_layers(): pl.pallas_call(layers_kernel, in_specs=[ANY] + [HBM] * 6, out_specs=[HBM]...  17.8 us
    all_to_all x1, starting transfers between devices, on_device(): received = exchange(to_blocks(input_field, cotangent), everyone)  11.7 us
    pallas_call x1, Pallas kernels, weight_gradients(): pl.pallas_call(functools.partial(weight_kernel, scale), in_specs=[pl.Bloc...  9.69 us
    pallas_call x1, Pallas kernels, prepare(): pl.pallas_call(functools.partial(prepare_kernel, scale), in_specs=[VMEM]...  8.88 us
    all_to_all x1, starting transfers between devices, on_device(): exchange(grad.reshape(groups * bricks, steps * J, LANES), everyone)  5.01 us
  transfers between devices with their start and end apart: 12, of which 5 were waited for; matrix products, arithmetic and copies ran while one was open for 0% of the time, Pallas kernels for 15%

profile of v4, /device:TPU:0, one launch (start us, length us, event | category | flops | bytes accessed | tf_op | source)
XLA Modules:
  0.0 141.1 jit_solution(15007687068240293612)
XLA Ops:
  0.6 4.0 %shard_map.76 = f32[128,64,128]{2,1,0:T(8,128)} custom-call(f32[4,32,4,1024]{3,2,1,0:T(4,128)} %first_any.1, f32[4,32,4,1024]{3,2,1,0:T(4,128)} %second_any.1), custom_call_target="tpu_custom_call" | custom-call | tf_op jit(solution)/shard_map/pallas_call | solution.py:114
  4.7 0.0 copy-start.2
  4.7 0.0 copy-start
  4.7 0.0 copy-start.1
  4.7 11.7 %all-to-all-start = ((f32[128,64,128]{2,1,0:T(8,128)}), f32[128,64,128]{2,1,0:T(8,128)}, u32[]{:S(2)}, u32[]{:S(2)}) async-start(f32[128,64,128]{2,1,0:T(8,128)} %shard_map.76), calls=%async_computation | async-start | bytes 8388608 | tf_op jit(solution)/shard_map/all_to_all | solution.py:611
  16.4 0.0 copy-done.2
  16.4 0.1 fusion.6
  16.6 0.1 copy.11
  16.7 0.0 copy-done
  16.7 0.0 copy-done.1
  16.7 8.9 %shard_map.77 = (bf16[2,256,512]{2,1,0:T(8,128)(2,1)}, bf16[2,512,256]{2,1,0:T(8,128)(2,1)}, bf16[2,2,16,32,256]{4,3,2,1,0:T(8,128)(2,1)}, bf16[2,2,16,32,256]{4...) custom-call(f32[32,64]{1,0:T(8,128)S(1)} %bitcast.7, f32[64,32]{1,0:T(8,128)S(1)} %bitcast.8, ...), custom_call_target="tpu_custom_call" | custom-call | tf_op jit(solution)/shard_map/pallas_call | solution.py:213
  25.6 43.0 %all-to-all-done = f32[128,64,128]{2,1,0:T(8,128)} async-done(((f32[128,64,128]{2,1,0:T(8,128)}), f32[128,64,128]{2,1,0:T(8,128)}, u32[]{:S(2)}, u32[]{:S(2)}) %all-to-all-start) | async-done | bytes 4194336 | tf_op jit(solution)/shard_map/all_to_all | solution.py:611
  68.5 17.8 %shard_map.78 = (f32[16,8,32,128]{3,2,1,0:T(8,128)}, f32[8,256,128]{2,1,0:T(8,128)}, f32[8,256,128]{2,1,0:T(8,128)}, f32[8,256,128]{2,1,0:T(8,128)}, f32[8,256,1...) custom-call(f32[16,8,64,128]{3,2,1,0:T(8,128)} %bitcast.2.refs_0_, ...), custom_call_target="tpu_custom_call" | custom-call | tf_op jit(solution)/shard_map/pallas_call | solution.py:415
  86.3 5.0 %all-to-all-start.1 = ((f32[128,32,128]{2,1,0:T(8,128)}), f32[128,32,128]{2,1,0:T(8,128)S(1)}, u32[]{:S(2)}, u32[]{:S(2)}) async-start(f32[128,32,128]{2,1,0:T(8,128)} %bitcast.9), calls=%async_computation.1 | async-start | bytes 4194304 | tf_op jit(solution)/shard_map/all_to_all | solution.py:617
  91.3 0.1 pad_add_fusion.me_ref
  91.4 9.7 %shard_map.80 = (f32[176,128]{1,0:T(8,128)S(1)}, f32[176,128]{1,0:T(8,128)S(1)}, f32[176,128]{1,0:T(8,128)S(1)}, f32[176,128]{1,0:T(8,128)S(1)}) custom-call(s32[2]{0:T(128)S(1)} %pad_add_fusion.me_ref, f32[8,256,128]{2,1,0:T(8,128)} %get-tuple-element.58.refs_0_, f32[8,256,128]{2,1,0:T(8,128)} %get-tuple-element.59.refs_1_, ...), custom_call_target="tpu_custom_call" | custom-call | tf_op jit(solution)/shard_map/pallas_call | solution.py:520
  101.1 1.0 collective-permute-start
  102.1 2.7 %collective-permute-start.1 = (f32[176,128]{1,0:T(8,128)S(1)}, f32[176,128]{1,0:T(8,128)S(1)}, u32[]{:S(2)}, u32[]{:S(2)}) collective-permute-start(f32[176,128]{1,0:T(8,128)S(1)} %get-tuple-element.72), channel_id=1, source_target_pairs={{0,64},{8,72},{16,80},{24,88},{32,96},{40,104},{48,112},{56,120},{... | collective-permute-start | bytes 270344 | tf_op jit(solution)/shard_map/ppermute | solution.py:543
  104.8 1.5 %collective-permute-start.2 = (f32[176,128]{1,0:T(8,128)S(1)}, f32[176,128]{1,0:T(8,128)S(1)}, u32[]{:S(2)}, u32[]{:S(2)}) collective-permute-start(f32[176,128]{1,0:T(8,128)S(1)} %get-tuple-element.73), channel_id=1, source_target_pairs={{0,96},{8,104},{16,112},{24,120},{32,0},{40,8},{48,16},{56,24},{64... | collective-permute-start | bytes 270344 | tf_op jit(solution)/shard_map/ppermute | solution.py:543
  106.3 12.1 %collective-permute-done.refs_1_ = f32[176,128]{1,0:T(8,128)S(1)} collective-permute-done((f32[176,128]{1,0:T(8,128)S(1)}, f32[176,128]{1,0:T(8,128)S(1)}, u32[]{:S(2)}, u32[]{:S(2)}) %collective-permute-start) | collective-permute-done | bytes 90144 | tf_op jit(solution)/shard_map/ppermute | solution.py:543
  118.4 2.0 %collective-permute-done.1.refs_2_ = f32[176,128]{1,0:T(8,128)S(1)} collective-permute-done((f32[176,128]{1,0:T(8,128)S(1)}, f32[176,128]{1,0:T(8,128)S(1)}, u32[]{:S(2)}, u32[]{:S(2)}) %collective-permute-start.1) | collective-permute-done | bytes 90144 | tf_op jit(solution)/shard_map/ppermute | solution.py:543
  120.4 0.0 collective-permute-done.2.refs_3_
  120.5 0.1 collective-permute-start.3
  120.6 1.5 %collective-permute-start.4 = (f32[80,128]{1,0:T(8,128)S(1)}, f32[80,128]{1,0:T(8,128)S(1)}, u32[]{:S(2)}, u32[]{:S(2)}) collective-permute-start(f32[80,128]{1,0:T(8,128)S(1)} %get-tuple-element.76), channel_id=1, source_target_pairs={{0,16},{8,24},{16,0},{24,8},{32,48},{40,56},{48,32},{56,40},{64,80... | collective-permute-start | bytes 122888 | tf_op jit(solution)/shard_map/ppermute | solution.py:543
  122.1 1.4 collective-permute-start.5
  123.5 0.0 all-to-all-done.1.blocks_any
  123.5 2.4 %shard_map.79 = f32[4,32,4,1024]{3,2,1,0:T(4,128)} custom-call(f32[128,32,128]{2,1,0:T(8,128)S(1)} %all-to-all-done.1.blocks_any), custom_call_target="tpu_custom_call" | custom-call | tf_op jit(solution)/shard_map/pallas_call | solution.py:132
  125.8 0.0 collective-permute-done.3
  125.9 0.0 collective-permute-done.4
  125.9 0.0 collective-permute-done.5
  125.9 3.5 %collective-permute-start.6 = (f32[80,128]{1,0:T(8,128)S(1)}, f32[80,128]{1,0:T(8,128)S(1)}, u32[]{:S(2)}, u32[]{:S(2)}) collective-permute-start(f32[80,128]{1,0:T(8,128)S(1)} %add_add_fusion.1), channel_id=1, source_target_pairs={{0,4},{1,5},{2,6},{3,7},{4,0},{5,1},{6,2},{7,3},{8,12},{9,13},{10,... | collective-permute-start | bytes 122888 | tf_op jit(solution)/shard_map/ppermute | solution.py:543
  129.4 0.8 collective-permute-start.7
  130.3 2.4 %collective-permute-start.8 = (f32[80,128]{1,0:T(8,128)S(1)}, f32[80,128]{1,0:T(8,128)S(1)}, u32[]{:S(2)}, u32[]{:S(2)}) collective-permute-start(f32[80,128]{1,0:T(8,128)S(1)} %add_add_fusion.1), channel_id=1, source_target_pairs={{0,6},{1,7},{2,0},{3,1},{4,2},{5,3},{6,4},{7,5},{8,14},{9,15},{10,... | collective-permute-start | bytes 122888 | tf_op jit(solution)/shard_map/ppermute | solution.py:543
  132.7 0.0 collective-permute-done.6
  132.7 2.0 %collective-permute-done.7 = f32[80,128]{1,0:T(8,128)S(1)} collective-permute-done((f32[80,128]{1,0:T(8,128)S(1)}, f32[80,128]{1,0:T(8,128)S(1)}, u32[]{:S(2)}, u32[]{:S(2)}) %collective-permute-start.7) | collective-permute-done | bytes 40992 | tf_op jit(solution)/shard_map/ppermute | solution.py:543
  134.6 0.0 collective-permute-done.8
  134.7 2.9 %collective-permute-start.9 = (f32[80,128]{1,0:T(8,128)S(1)}, f32[80,128]{1,0:T(8,128)S(1)}, u32[]{:S(2)}, u32[]{:S(2)}) collective-permute-start(f32[80,128]{1,0:T(8,128)S(1)} %add_add_fusion.one_ref), channel_id=1, source_target_pairs={{0,1},{1,0},{2,3},{3,2},{4,5},{5,4},{6,7},{7,6},{8,9},{9,8},{10,11... | collective-permute-start | bytes 122888 | tf_op jit(solution)/shard_map/ppermute | solution.py:543
  137.6 2.7 %collective-permute-done.9.other_ref = f32[80,128]{1,0:T(8,128)S(1)} collective-permute-done((f32[80,128]{1,0:T(8,128)S(1)}, f32[80,128]{1,0:T(8,128)S(1)}, u32[]{:S(2)}, u32[]{:S(2)}) %collective-permute-start.9) | collective-permute-done | bytes 40992 | tf_op jit(solution)/shard_map/ppermute | solution.py:543
  140.3 0.9 shard_map.82
  (5 shorter events, 0.1 us)
Async XLA Ops:
  4.7 11.7 %copy-start.2 = (s32[16]{0:T(128)S(1)}, s32[16]{0:T(128)}, u32[]{:S(2)}) copy-start(s32[16]{0:T(128)} %param.9) | copy-start | bytes 196
  4.7 12.0 %copy-start = (f32[2,2,16,32,32]{4,3,2,1,0:T(8,128)S(1)}, f32[2,2,16,32,32]{4,3,2,1,0:T(8,128)}, u32[]{:S(2)}) copy-start(f32[2,2,16,32,32]{4,3,2,1,0:T(8,128)} %w_ref.1) | copy-start | bytes 786436
  4.7 12.0 %copy-start.1 = (f32[2,3,32,32]{3,2,1,0:T(8,128)S(1)}, f32[2,3,32,32]{3,2,1,0:T(8,128)}, u32[]{:S(2)}) copy-start(f32[2,3,32,32]{3,2,1,0:T(8,128)} %k_ref.1) | copy-start | bytes 73732
  4.7 63.8 %all-to-all-start = ((f32[128,64,128]{2,1,0:T(8,128)}), f32[128,64,128]{2,1,0:T(8,128)}, u32[]{:S(2)}, u32[]{:S(2)}) async-start(f32[128,64,128]{2,1,0:T(8,128)} %shard_map.76), calls=%async_computation | async-start | bytes 8388608 | tf_op jit(solution)/shard_map/all_to_all | solution.py:611
  86.3 37.2 %all-to-all-start.1 = ((f32[128,32,128]{2,1,0:T(8,128)}), f32[128,32,128]{2,1,0:T(8,128)S(1)}, u32[]{:S(2)}, u32[]{:S(2)}) async-start(f32[128,32,128]{2,1,0:T(8,128)} %bitcast.9), calls=%async_computation.1 | async-start | bytes 4194304 | tf_op jit(solution)/shard_map/all_to_all | solution.py:617
  101.1 17.3 %collective-permute-start = (f32[176,128]{1,0:T(8,128)S(1)}, f32[176,128]{1,0:T(8,128)S(1)}, u32[]{:S(2)}, u32[]{:S(2)}) collective-permute-start(f32[176,128]{1,0:T(8,128)S(1)} %get-tuple-element.71), channel_id=1, source_target_pairs={{0,32},{8,40},{16,48},{24,56},{32,64},{40,72},{48,80},{56,88},{64,... | collective-permute-start | bytes 270344 | tf_op jit(solution)/shard_map/ppermute | solution.py:543
  102.1 18.3 %collective-permute-start.1 = (f32[176,128]{1,0:T(8,128)S(1)}, f32[176,128]{1,0:T(8,128)S(1)}, u32[]{:S(2)}, u32[]{:S(2)}) collective-permute-start(f32[176,128]{1,0:T(8,128)S(1)} %get-tuple-element.72), channel_id=1, source_target_pairs={{0,64},{8,72},{16,80},{24,88},{32,96},{40,104},{48,112},{56,120},{... | collective-permute-start | bytes 270344 | tf_op jit(solution)/shard_map/ppermute | solution.py:543
  104.8 15.6 %collective-permute-start.2 = (f32[176,128]{1,0:T(8,128)S(1)}, f32[176,128]{1,0:T(8,128)S(1)}, u32[]{:S(2)}, u32[]{:S(2)}) collective-permute-start(f32[176,128]{1,0:T(8,128)S(1)} %get-tuple-element.73), channel_id=1, source_target_pairs={{0,96},{8,104},{16,112},{24,120},{32,0},{40,8},{48,16},{56,24},{64... | collective-permute-start | bytes 270344 | tf_op jit(solution)/shard_map/ppermute | solution.py:543
  120.5 5.4 %collective-permute-start.3 = (f32[80,128]{1,0:T(8,128)S(1)}, f32[80,128]{1,0:T(8,128)S(1)}, u32[]{:S(2)}, u32[]{:S(2)}) collective-permute-start(f32[80,128]{1,0:T(8,128)S(1)} %get-tuple-element.75), channel_id=1, source_target_pairs={{0,8},{8,16},{16,24},{24,0},{32,40},{40,48},{48,56},{56,32},{64,72... | collective-permute-start | bytes 122888 | tf_op jit(solution)/shard_map/ppermute | solution.py:543
  120.6 5.3 %collective-permute-start.4 = (f32[80,128]{1,0:T(8,128)S(1)}, f32[80,128]{1,0:T(8,128)S(1)}, u32[]{:S(2)}, u32[]{:S(2)}) collective-permute-start(f32[80,128]{1,0:T(8,128)S(1)} %get-tuple-element.76), channel_id=1, source_target_pairs={{0,16},{8,24},{16,0},{24,8},{32,48},{40,56},{48,32},{56,40},{64,80... | collective-permute-start | bytes 122888 | tf_op jit(solution)/shard_map/ppermute | solution.py:543
  122.1 3.8 %collective-permute-start.5 = (f32[80,128]{1,0:T(8,128)S(1)}, f32[80,128]{1,0:T(8,128)S(1)}, u32[]{:S(2)}, u32[]{:S(2)}) collective-permute-start(f32[80,128]{1,0:T(8,128)S(1)} %get-tuple-element.77), channel_id=1, source_target_pairs={{0,24},{8,0},{16,8},{24,16},{32,56},{40,32},{48,40},{56,48},{64,88... | collective-permute-start | bytes 122888 | tf_op jit(solution)/shard_map/ppermute | solution.py:543
  125.9 6.8 %collective-permute-start.6 = (f32[80,128]{1,0:T(8,128)S(1)}, f32[80,128]{1,0:T(8,128)S(1)}, u32[]{:S(2)}, u32[]{:S(2)}) collective-permute-start(f32[80,128]{1,0:T(8,128)S(1)} %add_add_fusion.1), channel_id=1, source_target_pairs={{0,4},{1,5},{2,6},{3,7},{4,0},{5,1},{6,2},{7,3},{8,12},{9,13},{10,... | collective-permute-start | bytes 122888 | tf_op jit(solution)/shard_map/ppermute | solution.py:543
  129.4 5.2 %collective-permute-start.7 = (f32[80,128]{1,0:T(8,128)S(1)}, f32[80,128]{1,0:T(8,128)S(1)}, u32[]{:S(2)}, u32[]{:S(2)}) collective-permute-start(f32[80,128]{1,0:T(8,128)S(1)} %add_add_fusion.1), channel_id=1, source_target_pairs={{0,2},{1,3},{2,4},{3,5},{4,6},{5,7},{6,0},{7,1},{8,10},{9,11},{10,... | collective-permute-start | bytes 122888 | tf_op jit(solution)/shard_map/ppermute | solution.py:543
  130.3 4.4 %collective-permute-start.8 = (f32[80,128]{1,0:T(8,128)S(1)}, f32[80,128]{1,0:T(8,128)S(1)}, u32[]{:S(2)}, u32[]{:S(2)}) collective-permute-start(f32[80,128]{1,0:T(8,128)S(1)} %add_add_fusion.1), channel_id=1, source_target_pairs={{0,6},{1,7},{2,0},{3,1},{4,2},{5,3},{6,4},{7,5},{8,14},{9,15},{10,... | collective-permute-start | bytes 122888 | tf_op jit(solution)/shard_map/ppermute | solution.py:543
  134.7 5.6 %collective-permute-start.9 = (f32[80,128]{1,0:T(8,128)S(1)}, f32[80,128]{1,0:T(8,128)S(1)}, u32[]{:S(2)}, u32[]{:S(2)}) collective-permute-start(f32[80,128]{1,0:T(8,128)S(1)} %add_add_fusion.one_ref), channel_id=1, source_target_pairs={{0,1},{1,0},{2,3},{3,2},{4,5},{5,4},{6,7},{7,6},{8,9},{9,8},{10,11... | collective-permute-start | bytes 122888 | tf_op jit(solution)/shard_map/ppermute | solution.py:543

commit v5 on v4

--- a/solution.py
+++ b/solution.py
@@ -619,11 +619,14 @@
     place = jnp.stack([me // RADIX, me % RADIX])
     pieces = weight_gradients(scale, place, *kept)
     pieces = split_sum(shifted(pieces, "tm", groups, RADIX))
+    total = ring_sum(shifted(pieces, "tm", groups, 1))
     grad_input, pieces = lax.optimization_barrier(
-        (from_blocks(returned), shifted(pieces, "tm", groups, 1))
+        (
+            from_blocks(returned),
+            shifted([total] * RADIX, "space", bricks, bricks // RADIX),
+        )
     )
     total = ring_sum(pieces)
-    total = ring_sum(shifted([total] * RADIX, "space", bricks, bricks // RADIX))
     mode_total, kernel_total = finish(*shifted([total] * 2, "space", bricks, 1), layers)
     return (grad_input, mode_total, kernel_total)
 

time: 141 us -> 141 us (level)
  transfers between devices with their start and end apart: 12 -> 12, of which waited for: 5 -> 7; matrix products, arithmetic and copies ran while one was open for 0% -> 0% of each run, Pallas kernels for 15% -> 15%
where the time goes in v5:
time: 141 us
  waiting for transfers between devices  62 us (44%)
  Pallas kernels  43.6 us (31%)
  starting transfers between devices  34.2 us (24%)
    all_to_all x1, waiting for transfers between devices, on_device(): received = exchange(to_blocks(input_field, cotangent), everyone)  43 us
    ppermute x10, waiting for transfers between devices, shifted(): got.append(lax.ppermute(pieces[r], axis, perm))  19 us
    pallas_call x1, Pallas kernels, run_layers(): pl.pallas_call(layers_kernel, in_specs=[ANY] + [HBM] * 6, out_specs=[HBM]...  17.8 us
    ppermute x10, starting transfers between devices, shifted(): got.append(lax.ppermute(pieces[r], axis, perm))  17.5 us
    all_to_all x1, starting transfers between devices, on_device(): received = exchange(to_blocks(input_field, cotangent), everyone)  11.7 us
    pallas_call x1, Pallas kernels, weight_gradients(): pl.pallas_call(functools.partial(weight_kernel, scale), in_specs=[pl.Bloc...  9.69 us
    pallas_call x1, Pallas kernels, prepare(): pl.pallas_call(functools.partial(prepare_kernel, scale), in_specs=[VMEM]...  8.88 us
    all_to_all x1, starting transfers between devices, on_device(): exchange(grad.reshape(groups * bricks, steps * J, LANES), everyone)  5.01 us
  transfers between devices with their start and end apart: 12, of which 7 were waited for; matrix products, arithmetic and copies ran while one was open for 0% of the time, Pallas kernels for 15%

profile of v5, /device:TPU:0, one launch (start us, length us, event | category | flops | bytes accessed | tf_op | source)
XLA Modules:
  0.0 140.9 jit_solution(14765917282020139067)
XLA Ops:
  0.6 4.0 %shard_map.76 = f32[128,64,128]{2,1,0:T(8,128)} custom-call(f32[4,32,4,1024]{3,2,1,0:T(4,128)} %first_any.1, f32[4,32,4,1024]{3,2,1,0:T(4,128)} %second_any.1), custom_call_target="tpu_custom_call" | custom-call | tf_op jit(solution)/shard_map/pallas_call | solution.py:114
  4.7 0.0 copy-start.2
  4.7 0.0 copy-start
  4.7 0.0 copy-start.1
  4.7 11.7 %all-to-all-start = ((f32[128,64,128]{2,1,0:T(8,128)}), f32[128,64,128]{2,1,0:T(8,128)}, u32[]{:S(2)}, u32[]{:S(2)}) async-start(f32[128,64,128]{2,1,0:T(8,128)} %shard_map.76), calls=%async_computation | async-start | bytes 8388608 | tf_op jit(solution)/shard_map/all_to_all | solution.py:611
  16.4 0.0 copy-done.2
  16.4 0.1 fusion.6
  16.6 0.1 copy.11
  16.7 0.0 copy-done
  16.7 0.0 copy-done.1
  16.7 8.9 %shard_map.77 = (bf16[2,256,512]{2,1,0:T(8,128)(2,1)}, bf16[2,512,256]{2,1,0:T(8,128)(2,1)}, bf16[2,2,16,32,256]{4,3,2,1,0:T(8,128)(2,1)}, bf16[2,2,16,32,256]{4...) custom-call(f32[32,64]{1,0:T(8,128)S(1)} %bitcast.7, f32[64,32]{1,0:T(8,128)S(1)} %bitcast.8, ...), custom_call_target="tpu_custom_call" | custom-call | tf_op jit(solution)/shard_map/pallas_call | solution.py:213
  25.6 43.0 %all-to-all-done = f32[128,64,128]{2,1,0:T(8,128)} async-done(((f32[128,64,128]{2,1,0:T(8,128)}), f32[128,64,128]{2,1,0:T(8,128)}, u32[]{:S(2)}, u32[]{:S(2)}) %all-to-all-start) | async-done | bytes 4194336 | tf_op jit(solution)/shard_map/all_to_all | solution.py:611
  68.5 17.8 %shard_map.78 = (f32[16,8,32,128]{3,2,1,0:T(8,128)}, f32[8,256,128]{2,1,0:T(8,128)}, f32[8,256,128]{2,1,0:T(8,128)}, f32[8,256,128]{2,1,0:T(8,128)}, f32[8,256,1...) custom-call(f32[16,8,64,128]{3,2,1,0:T(8,128)} %bitcast.2.refs_0_, ...), custom_call_target="tpu_custom_call" | custom-call | tf_op jit(solution)/shard_map/pallas_call | solution.py:415
  86.3 5.0 %all-to-all-start.1 = ((f32[128,32,128]{2,1,0:T(8,128)}), f32[128,32,128]{2,1,0:T(8,128)S(1)}, u32[]{:S(2)}, u32[]{:S(2)}) async-start(f32[128,32,128]{2,1,0:T(8,128)} %bitcast.9), calls=%async_computation.1 | async-start | bytes 4194304 | tf_op jit(solution)/shard_map/all_to_all | solution.py:617
  91.3 0.1 pad_add_fusion.me_ref
  91.4 9.7 %shard_map.80 = (f32[176,128]{1,0:T(8,128)S(1)}, f32[176,128]{1,0:T(8,128)S(1)}, f32[176,128]{1,0:T(8,128)S(1)}, f32[176,128]{1,0:T(8,128)S(1)}) custom-call(s32[2]{0:T(128)S(1)} %pad_add_fusion.me_ref, f32[8,256,128]{2,1,0:T(8,128)} %get-tuple-element.58.refs_0_, f32[8,256,128]{2,1,0:T(8,128)} %get-tuple-element.59.refs_1_, ...), custom_call_target="tpu_custom_call" | custom-call | tf_op jit(solution)/shard_map/pallas_call | solution.py:520
  101.1 1.0 collective-permute-start
  102.1 2.7 %collective-permute-start.1 = (f32[176,128]{1,0:T(8,128)S(1)}, f32[176,128]{1,0:T(8,128)S(1)}, u32[]{:S(2)}, u32[]{:S(2)}) collective-permute-start(f32[176,128]{1,0:T(8,128)S(1)} %get-tuple-element.72), channel_id=1, source_target_pairs={{0,64},{8,72},{16,80},{24,88},{32,96},{40,104},{48,112},{56,120},{... | collective-permute-start | bytes 270344 | tf_op jit(solution)/shard_map/ppermute | solution.py:543
  104.8 1.5 %collective-permute-start.2 = (f32[176,128]{1,0:T(8,128)S(1)}, f32[176,128]{1,0:T(8,128)S(1)}, u32[]{:S(2)}, u32[]{:S(2)}) collective-permute-start(f32[176,128]{1,0:T(8,128)S(1)} %get-tuple-element.73), channel_id=1, source_target_pairs={{0,96},{8,104},{16,112},{24,120},{32,0},{40,8},{48,16},{56,24},{64... | collective-permute-start | bytes 270344 | tf_op jit(solution)/shard_map/ppermute | solution.py:543
  106.3 12.1 %collective-permute-done.refs_1_ = f32[176,128]{1,0:T(8,128)S(1)} collective-permute-done((f32[176,128]{1,0:T(8,128)S(1)}, f32[176,128]{1,0:T(8,128)S(1)}, u32[]{:S(2)}, u32[]{:S(2)}) %collective-permute-start) | collective-permute-done | bytes 90144 | tf_op jit(solution)/shard_map/ppermute | solution.py:543
  118.4 2.0 %collective-permute-done.1.refs_2_ = f32[176,128]{1,0:T(8,128)S(1)} collective-permute-done((f32[176,128]{1,0:T(8,128)S(1)}, f32[176,128]{1,0:T(8,128)S(1)}, u32[]{:S(2)}, u32[]{:S(2)}) %collective-permute-start.1) | collective-permute-done | bytes 90144 | tf_op jit(solution)/shard_map/ppermute | solution.py:543
  120.4 0.0 collective-permute-done.2.refs_3_
  120.5 1.5 %collective-permute-start.3 = (f32[80,128]{1,0:T(8,128)S(1)}, f32[80,128]{1,0:T(8,128)S(1)}, u32[]{:S(2)}, u32[]{:S(2)}) collective-permute-start(f32[80,128]{1,0:T(8,128)S(1)} %get-tuple-element.75), channel_id=1, source_target_pairs={{0,16},{8,24},{16,0},{24,8},{32,48},{40,56},{48,32},{56,40},{64,80... | collective-permute-start | bytes 122888 | tf_op jit(solution)/shard_map/ppermute | solution.py:543
  122.0 0.0 collective-permute-start.4
  122.0 1.7 %collective-permute-start.5 = (f32[80,128]{1,0:T(8,128)S(1)}, f32[80,128]{1,0:T(8,128)S(1)}, u32[]{:S(2)}, u32[]{:S(2)}) collective-permute-start(f32[80,128]{1,0:T(8,128)S(1)} %get-tuple-element.77), channel_id=1, source_target_pairs={{0,24},{8,0},{16,8},{24,16},{32,56},{40,32},{48,40},{56,48},{64,88... | collective-permute-start | bytes 122888 | tf_op jit(solution)/shard_map/ppermute | solution.py:543
  123.8 0.8 collective-permute-done.3
  124.6 0.9 collective-permute-done.4
  125.4 0.0 collective-permute-done.5
  125.5 1.7 %collective-permute-start.6 = (f32[80,128]{1,0:T(8,128)S(1)}, f32[80,128]{1,0:T(8,128)S(1)}, u32[]{:S(2)}, u32[]{:S(2)}) collective-permute-start(f32[80,128]{1,0:T(8,128)S(1)} %add_add_fusion.1), channel_id=1, source_target_pairs={{0,2},{1,3},{2,4},{3,5},{4,6},{5,7},{6,0},{7,1},{8,10},{9,11},{10,... | collective-permute-start | bytes 122888 | tf_op jit(solution)/shard_map/ppermute | solution.py:543
  127.2 3.2 %collective-permute-start.7 = (f32[80,128]{1,0:T(8,128)S(1)}, f32[80,128]{1,0:T(8,128)S(1)}, u32[]{:S(2)}, u32[]{:S(2)}) collective-permute-start(f32[80,128]{1,0:T(8,128)S(1)} %add_add_fusion.1), channel_id=1, source_target_pairs={{0,4},{1,5},{2,6},{3,7},{4,0},{5,1},{6,2},{7,3},{8,12},{9,13},{10,... | collective-permute-start | bytes 122888 | tf_op jit(solution)/shard_map/ppermute | solution.py:543
  130.4 1.2 collective-permute-start.8
  131.6 0.0 all-to-all-done.1.blocks_any
  131.6 2.4 %shard_map.79 = f32[4,32,4,1024]{3,2,1,0:T(4,128)} custom-call(f32[128,32,128]{2,1,0:T(8,128)S(1)} %all-to-all-done.1.blocks_any), custom_call_target="tpu_custom_call" | custom-call | tf_op jit(solution)/shard_map/pallas_call | solution.py:132
  134.0 0.0 collective-permute-done.6
  134.0 0.0 collective-permute-done.7
  134.0 0.4 collective-permute-done.8
  134.4 2.9 %collective-permute-start.9 = (f32[80,128]{1,0:T(8,128)S(1)}, f32[80,128]{1,0:T(8,128)S(1)}, u32[]{:S(2)}, u32[]{:S(2)}) collective-permute-start(f32[80,128]{1,0:T(8,128)S(1)} %add_add_fusion.one_ref), channel_id=1, source_target_pairs={{0,1},{1,0},{2,3},{3,2},{4,5},{5,4},{6,7},{7,6},{8,9},{9,8},{10,11... | collective-permute-start | bytes 122888 | tf_op jit(solution)/shard_map/ppermute | solution.py:543
  137.3 2.7 %collective-permute-done.9.other_ref = f32[80,128]{1,0:T(8,128)S(1)} collective-permute-done((f32[80,128]{1,0:T(8,128)S(1)}, f32[80,128]{1,0:T(8,128)S(1)}, u32[]{:S(2)}, u32[]{:S(2)}) %collective-permute-start.9) | collective-permute-done | bytes 40992 | tf_op jit(solution)/shard_map/ppermute | solution.py:543
  140.0 0.9 shard_map.82
  (5 shorter events, 0.1 us)
Async XLA Ops:
  4.7 11.7 %copy-start.2 = (s32[16]{0:T(128)S(1)}, s32[16]{0:T(128)}, u32[]{:S(2)}) copy-start(s32[16]{0:T(128)} %param.9) | copy-start | bytes 196
  4.7 12.0 %copy-start = (f32[2,2,16,32,32]{4,3,2,1,0:T(8,128)S(1)}, f32[2,2,16,32,32]{4,3,2,1,0:T(8,128)}, u32[]{:S(2)}) copy-start(f32[2,2,16,32,32]{4,3,2,1,0:T(8,128)} %w_ref.1) | copy-start | bytes 786436
  4.7 12.0 %copy-start.1 = (f32[2,3,32,32]{3,2,1,0:T(8,128)S(1)}, f32[2,3,32,32]{3,2,1,0:T(8,128)}, u32[]{:S(2)}) copy-start(f32[2,3,32,32]{3,2,1,0:T(8,128)} %k_ref.1) | copy-start | bytes 73732
  4.7 63.8 %all-to-all-start = ((f32[128,64,128]{2,1,0:T(8,128)}), f32[128,64,128]{2,1,0:T(8,128)}, u32[]{:S(2)}, u32[]{:S(2)}) async-start(f32[128,64,128]{2,1,0:T(8,128)} %shard_map.76), calls=%async_computation | async-start | bytes 8388608 | tf_op jit(solution)/shard_map/all_to_all | solution.py:611
  86.3 45.3 %all-to-all-start.1 = ((f32[128,32,128]{2,1,0:T(8,128)}), f32[128,32,128]{2,1,0:T(8,128)S(1)}, u32[]{:S(2)}, u32[]{:S(2)}) async-start(f32[128,32,128]{2,1,0:T(8,128)} %bitcast.9), calls=%async_computation.1 | async-start | bytes 4194304 | tf_op jit(solution)/shard_map/all_to_all | solution.py:617
  101.1 17.3 %collective-permute-start = (f32[176,128]{1,0:T(8,128)S(1)}, f32[176,128]{1,0:T(8,128)S(1)}, u32[]{:S(2)}, u32[]{:S(2)}) collective-permute-start(f32[176,128]{1,0:T(8,128)S(1)} %get-tuple-element.71), channel_id=1, source_target_pairs={{0,32},{8,40},{16,48},{24,56},{32,64},{40,72},{48,80},{56,88},{64,... | collective-permute-start | bytes 270344 | tf_op jit(solution)/shard_map/ppermute | solution.py:543
  102.1 18.3 %collective-permute-start.1 = (f32[176,128]{1,0:T(8,128)S(1)}, f32[176,128]{1,0:T(8,128)S(1)}, u32[]{:S(2)}, u32[]{:S(2)}) collective-permute-start(f32[176,128]{1,0:T(8,128)S(1)} %get-tuple-element.72), channel_id=1, source_target_pairs={{0,64},{8,72},{16,80},{24,88},{32,96},{40,104},{48,112},{56,120},{... | collective-permute-start | bytes 270344 | tf_op jit(solution)/shard_map/ppermute | solution.py:543
  104.8 15.6 %collective-permute-start.2 = (f32[176,128]{1,0:T(8,128)S(1)}, f32[176,128]{1,0:T(8,128)S(1)}, u32[]{:S(2)}, u32[]{:S(2)}) collective-permute-start(f32[176,128]{1,0:T(8,128)S(1)} %get-tuple-element.73), channel_id=1, source_target_pairs={{0,96},{8,104},{16,112},{24,120},{32,0},{40,8},{48,16},{56,24},{64... | collective-permute-start | bytes 270344 | tf_op jit(solution)/shard_map/ppermute | solution.py:543
  120.5 4.1 %collective-permute-start.3 = (f32[80,128]{1,0:T(8,128)S(1)}, f32[80,128]{1,0:T(8,128)S(1)}, u32[]{:S(2)}, u32[]{:S(2)}) collective-permute-start(f32[80,128]{1,0:T(8,128)S(1)} %get-tuple-element.75), channel_id=1, source_target_pairs={{0,16},{8,24},{16,0},{24,8},{32,48},{40,56},{48,32},{56,40},{64,80... | collective-permute-start | bytes 122888 | tf_op jit(solution)/shard_map/ppermute | solution.py:543
  122.0 3.4 %collective-permute-start.4 = (f32[80,128]{1,0:T(8,128)S(1)}, f32[80,128]{1,0:T(8,128)S(1)}, u32[]{:S(2)}, u32[]{:S(2)}) collective-permute-start(f32[80,128]{1,0:T(8,128)S(1)} %get-tuple-element.76), channel_id=1, source_target_pairs={{0,8},{8,16},{16,24},{24,0},{32,40},{40,48},{48,56},{56,32},{64,72... | collective-permute-start | bytes 122888 | tf_op jit(solution)/shard_map/ppermute | solution.py:543
  122.0 3.4 %collective-permute-start.5 = (f32[80,128]{1,0:T(8,128)S(1)}, f32[80,128]{1,0:T(8,128)S(1)}, u32[]{:S(2)}, u32[]{:S(2)}) collective-permute-start(f32[80,128]{1,0:T(8,128)S(1)} %get-tuple-element.77), channel_id=1, source_target_pairs={{0,24},{8,0},{16,8},{24,16},{32,56},{40,32},{48,40},{56,48},{64,88... | collective-permute-start | bytes 122888 | tf_op jit(solution)/shard_map/ppermute | solution.py:543
  125.5 8.5 %collective-permute-start.6 = (f32[80,128]{1,0:T(8,128)S(1)}, f32[80,128]{1,0:T(8,128)S(1)}, u32[]{:S(2)}, u32[]{:S(2)}) collective-permute-start(f32[80,128]{1,0:T(8,128)S(1)} %add_add_fusion.1), channel_id=1, source_target_pairs={{0,2},{1,3},{2,4},{3,5},{4,6},{5,7},{6,0},{7,1},{8,10},{9,11},{10,... | collective-permute-start | bytes 122888 | tf_op jit(solution)/shard_map/ppermute | solution.py:543
  127.2 6.8 %collective-permute-start.7 = (f32[80,128]{1,0:T(8,128)S(1)}, f32[80,128]{1,0:T(8,128)S(1)}, u32[]{:S(2)}, u32[]{:S(2)}) collective-permute-start(f32[80,128]{1,0:T(8,128)S(1)} %add_add_fusion.1), channel_id=1, source_target_pairs={{0,4},{1,5},{2,6},{3,7},{4,0},{5,1},{6,2},{7,3},{8,12},{9,13},{10,... | collective-permute-start | bytes 122888 | tf_op jit(solution)/shard_map/ppermute | solution.py:543
  130.4 4.0 %collective-permute-start.8 = (f32[80,128]{1,0:T(8,128)S(1)}, f32[80,128]{1,0:T(8,128)S(1)}, u32[]{:S(2)}, u32[]{:S(2)}) collective-permute-start(f32[80,128]{1,0:T(8,128)S(1)} %add_add_fusion.1), channel_id=1, source_target_pairs={{0,6},{1,7},{2,0},{3,1},{4,2},{5,3},{6,4},{7,5},{8,14},{9,15},{10,... | collective-permute-start | bytes 122888 | tf_op jit(solution)/shard_map/ppermute | solution.py:543
  134.4 5.6 %collective-permute-start.9 = (f32[80,128]{1,0:T(8,128)S(1)}, f32[80,128]{1,0:T(8,128)S(1)}, u32[]{:S(2)}, u32[]{:S(2)}) collective-permute-start(f32[80,128]{1,0:T(8,128)S(1)} %add_add_fusion.one_ref), channel_id=1, source_target_pairs={{0,1},{1,0},{2,3},{3,2},{4,5},{5,4},{6,7},{7,6},{8,9},{9,8},{10,11... | collective-permute-start | bytes 122888 | tf_op jit(solution)/shard_map/ppermute | solution.py:543
